TPU v7x, 128 devices: a whole 4x4x4 slice. The times are simulated.
128 devices in a mesh: slab: 8 (over z, core), tile: 16 (over y, x).
Axes of the slice: x: 4, y: 4, z: 4, core: 2. Of those that a mesh axis runs over, the one named last changes fastest.
Arguments:
- owner: int32 [32768, 1], P(('slab', 'tile')), may hold values from 0 to 127; in each aligned block of 256 rows (0 to 255, 256 to 511, ...) at most 4 rows name the same one
- block_base: int32 [3, 32768], P(None, ('slab', 'tile')), may hold values from 0 to 124, as said below
- spline_weights: float32 [12, 32768], P(None, ('slab', 'tile')), may hold values from 0.25 to 1
- measured: float32 [3, 32768], P(None, ('slab', 'tile')), may hold values from -6 to 6
- div_weight: float32 [1], replicated, may hold values from 0.05 to 0.5
- bend_weight: float32 [1], replicated, may hold values from 0.002 to 0.02
Outputs:
- solution: float32 [3, 32, 128, 128], P(None, 'slab', 'tile')
- residual: float32 [3, 32, 128, 128], P(None, 'slab', 'tile')
Inputs may be any that keep to these rules, and one draw needn't show every extreme that they name: `block_base`: row 0 is below 4, row 1 below 8, row 2 at most 124; each row reaches its largest value and 0. Among the 256 samples of one device at most 4 name the same owner.
All inputs are finite; a program needn't handle non-finite values.
Results may differ from a plain program's by a relative error of at most 0.0003.
Values sent between devices are 32-bit elements; how exact they have to be, the bound alone decides.
A program may use at most 64 MiB of HBM per device.

v0:
```python
import jax
import jax.numpy as jnp
from jax import lax
from jax.sharding import PartitionSpec as P

CZ = 4
CX = 8
NY = 128
S_DEV = 256
ITERS = 2


def passed_along(value, axis, steps):
    count = lax.axis_size(axis)
    initial, last = (max(0, -steps), min(count, count - steps))
    return lax.ppermute(value, axis, [(source, source + steps) for source in range(initial, last)])


def extended(block, sides, width):
    for axis, dim in sides:
        count = lax.axis_size(axis)
        forward = [(i, i + 1) for i in range(count - 1)]
        backward = [(target, source) for source, target in forward]
        low = lax.ppermute(
            lax.slice_in_dim(block, block.shape[dim] - width, None, axis=dim), axis, forward
        )
        high = lax.ppermute(lax.slice_in_dim(block, 0, width, axis=dim), axis, backward)
        block = jnp.concatenate([low, block, high], axis=dim)
    return block


def neighbours(field):
    middle = field[:, 1:-1, 1:-1, :]
    total = (
        field[:, 2:, 1:-1, :]
        + field[:, :-2, 1:-1, :]
        + field[:, 1:-1, 2:, :]
        + field[:, 1:-1, :-2, :]
    )
    padded = jnp.pad(middle, ((0, 0), (0, 0), (0, 0), (1, 1)))
    total = total + padded[..., 2:] + padded[..., :-2]
    return total - 6.0 * middle


def divergence(field):
    along_z = field[0, 2:, 1:-1, :] - field[0, 1:-1, 1:-1, :]
    along_x = field[1, 1:-1, 2:, :] - field[1, 1:-1, 1:-1, :]
    centre = field[2, 1:-1, 1:-1, :]
    along_y = jnp.pad(centre[..., 1:], ((0, 0), (0, 0), (0, 1))) - centre
    return along_z + along_x + along_y


def divergence_adjoint(values):
    centre = values[1:-1, 1:-1, :]
    first = values[:-2, 1:-1, :] - centre
    second = values[1:-1, :-2, :] - centre
    third = jnp.pad(centre[..., :-1], ((0, 0), (0, 0), (1, 0))) - centre
    return jnp.stack([first, second, third])


def squares(residual):
    return lax.psum(jnp.sum(residual * residual), ("slab", "tile"))


def placed(start, weights, count):
    cells = jnp.arange(count, dtype=jnp.int32)[None, :]
    total = jnp.zeros((start.shape[0], count), jnp.float32)
    for step in range(4):
        total = total + weights[step][:, None] * (cells == (start + step)[:, None]).astype(
            jnp.float32
        )
    return total


def local(owner, block_base, spline_weights, measured, div_weight, bend_weight):
    slabs = lax.axis_size("slab")
    tiles = lax.axis_size("tile")
    devices = slabs * tiles
    capacity = max(2, 2 * S_DEV // devices)
    target = owner[:, 0]
    onehot = (target[:, None] == jnp.arange(devices, dtype=jnp.int32)[None, :]).astype(jnp.int32)
    earlier = jnp.cumsum(onehot, axis=0) - onehot
    rank = jnp.sum(earlier * onehot, axis=1)
    place = target * capacity + rank
    payload = jnp.concatenate([spline_weights, measured], axis=0)
    outgoing = (
        jnp.zeros((15, devices * capacity), jnp.float32)
        .at[:, place]
        .set(payload)
        .reshape(15, devices, capacity)
    )
    offsets_out = (
        jnp.zeros((3, devices * capacity), jnp.int32)
        .at[:, place]
        .set(block_base)
        .reshape(3, devices, capacity)
    )
    arrived, located = (
        lax.all_to_all(outgoing, ("slab", "tile"), split_axis=1, concat_axis=1, tiled=True),
        lax.all_to_all(offsets_out, ("slab", "tile"), split_axis=1, concat_axis=1, tiled=True),
    )
    received = arrived.reshape(15, -1)
    located = located.reshape(3, -1)
    span_z = CZ + 6
    span_x = CX + 6
    weight_z = placed(located[0] + 3, received[0:4], span_z)
    weight_x = placed(located[1] + 3, received[4:8], span_x)
    weight_y = placed(located[2], received[8:12], NY)
    plane_weights = (weight_z[:, :, None] * weight_x[:, None, :]).reshape(-1, span_z * span_x)
    readings = received[12:15]
    rows_z = lax.axis_index("slab") * CZ + jnp.arange(CZ + 2, dtype=jnp.int32) - 1
    rows_x = lax.axis_index("tile") * CX + jnp.arange(CX + 2, dtype=jnp.int32) - 1
    inside = ((rows_z >= 0) & (rows_z < CZ * slabs))[:, None] & (
        (rows_x >= 0) & (rows_x < CX * tiles)
    )[None, :]
    inside = inside.astype(jnp.float32)[None, :, :, None]

    def spread(values):
        columns = (values.T[:, :, None] * weight_y[:, None, :]).reshape(-1, 3 * NY)
        total = lax.dot_general(
            plane_weights,
            columns,
            (((0,), (0,)), ((), ())),
            precision=lax.Precision.HIGHEST,
            preferred_element_type=jnp.float32,
        )
        total = total.reshape(span_z, span_x, 3, NY).transpose(2, 0, 1, 3)
        upper_x = total[:, :, CX + 3 :, :]
        lower_x = passed_along(upper_x, "tile", 1)
        total = total.at[:, :, 3:6, :].add(lower_x)
        upper_z = total[:, CZ + 3 :, 3 : CX + 3, :]
        lower_z = passed_along(upper_z, "slab", 1)
        total = total.at[:, 3:6, 3 : CX + 3, :].add(lower_z)
        return total[:, 3 : CZ + 3, 3 : CX + 3, :]

    right_side = spread(readings)
    solution = jnp.zeros_like(right_side)
    residual = right_side
    direction = right_side
    norm_now = squares(residual)
    for step in range(ITERS):
        operate_padded = extended(direction, (("slab", 1), ("tile", 2)), 3)
        grid = operate_padded.transpose(1, 2, 0, 3).reshape(span_z * span_x, 3 * NY)
        product = jnp.dot(
            plane_weights, grid, precision=lax.Precision.HIGHEST, preferred_element_type=jnp.float32
        )
        image = spread(jnp.sum(product.reshape(-1, 3, NY) * weight_y[:, None, :], axis=2).T)
        core = operate_padded[:, 2 : CZ + 4, 2 : CX + 4, :]
        smooth = neighbours(core)
        source = divergence(core)
        stacked = jnp.concatenate([smooth, source[None]], axis=0)
        wider = extended(stacked, (("slab", 1), ("tile", 2)), 1)
        bent = neighbours(wider[:3])
        pushed = divergence_adjoint(wider[3])
        image = image + div_weight[0] * pushed + bend_weight[0] * bent
        alpha = norm_now / lax.psum(jnp.sum(direction * image), ("slab", "tile"))
        solution = solution + alpha * direction
        residual = residual - alpha * image
        norm_next = squares(residual)
        direction = residual + norm_next / norm_now * direction
        norm_now = norm_next
    return (solution, residual)


def solution(mesh):
    placed = (
        P(("slab", "tile"), None),
        P(None, ("slab", "tile")),
        P(None, ("slab", "tile")),
        P(None, ("slab", "tile")),
        P(),
        P(),
    )
    return jax.shard_map(
        local,
        mesh=mesh,
        in_specs=placed,
        out_specs=(P(None, "slab", "tile", None), P(None, "slab", "tile", None)),
        check_vma=False,
    )
```

profile of v0, /device:TPU:1, one launch (start us, length us, event | category | flops | bytes accessed | tf_op | source)
XLA Modules:
  0.0 350.4 jit_solution(18175553264879759271)
XLA Ops:
  0.6 0.7 copy-done.1
  1.4 0.2 fusion.16
  1.7 0.2 fusion.18
  1.9 0.7 copy-done.2
  2.7 1.2 scatter_custom_fusion
  4.0 1.6 copy.47
  5.5 11.5 %all-to-all-start = ((s32[3,128,4]{2,0,1:T(4,128)}), s32[3,128,4]{2,0,1:T(4,128)S(1)}, u32[]{:S(2)}, u32[]{:S(2)}) async-start(s32[3,128,4]{2,0,1:T(4,128)} %copy.47), calls=%async_computation | async-start | bytes 524288 | tf_op jit(solution)/shard_map/all_to_all | solution.py:100
  17.2 1.8 scatter_custom_fusion.1
  19.0 9.3 %all-to-all-done = s32[3,128,4]{2,0,1:T(4,128)S(1)} async-done(((s32[3,128,4]{2,0,1:T(4,128)}), s32[3,128,4]{2,0,1:T(4,128)S(1)}, u32[]{:S(2)}, u32[]{:S(2)}) %all-to-all-start) | async-done | bytes 6176 | tf_op jit(solution)/shard_map/all_to_all | solution.py:100
  28.3 4.2 %all-to-all-start.1 = ((f32[15,128,4]{0,2,1:T(4,128)}), f32[15,128,4]{0,2,1:T(4,128)S(1)}, u32[]{:S(2)}, u32[]{:S(2)}) async-start(f32[15,128,4]{0,2,1:T(4,128)} %bitcast.10), calls=%async_computation.1 | async-start | bytes 524288 | tf_op jit(solution)/shard_map/all_to_all | solution.py:99
  32.5 1.6 add_reduce_fusion.7
  35.1 8.6 %all-to-all-done.1 = f32[15,128,4]{0,2,1:T(4,128)S(1)} async-done(((f32[15,128,4]{0,2,1:T(4,128)}), f32[15,128,4]{0,2,1:T(4,128)S(1)}, u32[]{:S(2)}, u32[]{:S(2)}) %all-to-all-start.1) | async-done | bytes 30752 | tf_op jit(solution)/shard_map/all_to_all | solution.py:99
  43.7 0.2 slice.686
  44.1 3.2 slice_reduce_fusion.11
  48.9 0.9 fusion.6
  49.8 2.2 collective-permute-start
  52.1 1.3 collective-permute-done
  53.3 0.3 scatter-add.20
  53.6 3.9 %collective-permute-start.1 = (f32[3,3,8,128]{3,2,1,0:T(8,128)S(1)}, f32[3,3,8,128]{3,2,1,0:T(8,128)S(1)}, u32[]{:S(2)}, u32[]{:S(2)}) collective-permute-start(f32[3,3,8,128]{3,2,1,0:T(8,128)S(1)} %copy.72), channel_id=1, source_target_pairs={{0,16},{16,32},{32,48},{48,64},{64,80},{80,96},{96,112},{1,17},{17... | collective-permute-start | bytes 110600 | tf_op jit(solution)/shard_map/ppermute | solution.py:16
  57.5 1.0 collective-permute-done.1
  58.8 4.2 %collective-permute-start.2 = (f32[3,3,8,128]{3,2,1,0:T(8,128)S(1)}, f32[3,3,8,128]{3,2,1,0:T(8,128)S(1)}, u32[]{:S(2)}, u32[]{:S(2)}) collective-permute-start(f32[3,3,8,128]{3,2,1,0:T(8,128)S(1)} %copy.74), channel_id=1, source_target_pairs={{0,16},{16,32},{32,48},{48,64},{64,80},{80,96},{96,112},{1,17},{17... | collective-permute-start | bytes 110600 | tf_op jit(solution)/shard_map/ppermute | solution.py:24
  64.3 1.9 collective-permute-start.3
  66.3 3.3 collective-permute-done.3
  69.7 1.3 collective-permute-start.5
  71.0 4.6 %collective-permute-start.4 = (f32[3,10,3,128]{3,2,1,0:T(4,128)S(1)}, f32[3,10,3,128]{3,2,1,0:T(4,128)S(1)}, u32[]{:S(2)}, u32[]{:S(2)}) collective-permute-start(f32[3,10,3,128]{3,2,1,0:T(4,128)S(1)} %get-tuple-element.107), channel_id=1, source_target_pairs={{0,1},{1,2},{2,3},{3,4},{4,5},{5,6},{6,7},{7,8},{8,9},{9,10},{10,1... | collective-permute-start | bytes 138248 | tf_op jit(solution)/shard_map/ppermute | solution.py:24
  75.7 1.2 collective-permute-done.4
  77.0 2.8 collective-permute-start.8
  79.8 2.1 collective-permute-start.9
  82.0 0.2 copy.55
  82.3 1.0 fusion.2
  83.3 1.6 collective-permute-done.9
  84.9 1.3 collective-permute-start.11
  86.2 4.6 %collective-permute-start.10 = (f32[4,6,1,128]{3,2,1,0:T(1,128)S(1)}, f32[4,6,1,128]{3,2,1,0:T(1,128)S(1)}, u32[]{:S(2)}, u32[]{:S(2)}) collective-permute-start(f32[4,6,1,128]{3,2,1,0:T(1,128)S(1)} %get-tuple-element.111), channel_id=1, source_target_pairs={{0,1},{1,2},{2,3},{3,4},{4,5},{5,6},{6,7},{7,8},{8,9},{9,10},{10,1... | collective-permute-start | bytes 36872 | tf_op jit(solution)/shard_map/ppermute | solution.py:24
  90.8 0.9 fusion.96
  91.7 3.6 %collective-permute-start.6 = (f32[3,10,3,128]{3,2,1,0:T(4,128)S(1)}, f32[3,10,3,128]{3,2,1,0:T(4,128)S(1)}, u32[]{:S(2)}, u32[]{:S(2)}) collective-permute-start(f32[3,10,3,128]{3,2,1,0:T(4,128)S(1)} %slice.701), channel_id=1, source_target_pairs={{0,1},{1,2},{2,3},{3,4},{4,5},{5,6},{6,7},{7,8},{8,9},{9,10},{10,1... | collective-permute-start | bytes 138248 | tf_op jit(solution)/shard_map/ppermute | solution.py:16
  95.4 1.2 collective-permute-done.6
  96.7 0.3 scatter-add.24
  97.0 3.2 collective-permute-start.7
  100.3 1.0 collective-permute-done.7
  101.4 0.7 multiply_reduce_fusion.2
  102.1 70.8 %all-reduce.8 = (f32[]{:T(128)}, f32[]{:T(128)}) all-reduce(f32[]{:T(128)} %get-tuple-element.96, f32[]{:T(128)} %get-tuple-element.95), channel_id=1, replica_groups=mesh['slab'=8,'tile'=16] {'slab','tile'}, use_global_device_ids=true, to_apply=%region_6.7 | all-reduce | flops 2 | bytes 16 | tf_op jit(solution)/shard_map/psum | solution.py:62
  174.3 0.6 multiply_reduce_fusion.1
  174.9 62.7 %psum.30 = f32[]{:T(128)} all-reduce(f32[]{:T(128)} %multiply_reduce_fusion.1), channel_id=1, replica_groups=mesh['slab'=8,'tile'=16] {'slab','tile'}, use_global_device_ids=true, to_apply=%region_11.12 | all-reduce | flops 1 | bytes 8 | tf_op jit(solution)/shard_map/psum | solution.py:62
  238.9 3.6 %collective-permute-start.12 = (f32[3,3,8,128]{3,2,1,0:T(8,128)S(1)}, f32[3,3,8,128]{3,2,1,0:T(8,128)S(1)}, u32[]{:S(2)}, u32[]{:S(2)}) collective-permute-start(f32[3,3,8,128]{3,2,1,0:T(8,128)S(1)} %get-tuple-element.121), channel_id=1, source_target_pairs={{0,16},{16,32},{32,48},{48,64},{64,80},{80,96},{96,112},{1,17},{17... | collective-permute-start | bytes 110600 | tf_op jit(solution)/shard_map/ppermute | solution.py:24
  242.5 1.9 collective-permute-start.13
  244.5 3.3 collective-permute-done.13
  247.9 1.3 collective-permute-start.15
  249.2 4.0 %collective-permute-start.14 = (f32[3,10,3,128]{3,2,1,0:T(4,128)S(1)}, f32[3,10,3,128]{3,2,1,0:T(4,128)S(1)}, u32[]{:S(2)}, u32[]{:S(2)}) collective-permute-start(f32[3,10,3,128]{3,2,1,0:T(4,128)S(1)} %get-tuple-element.105), channel_id=1, source_target_pairs={{0,1},{1,2},{2,3},{3,4},{4,5},{5,6},{6,7},{7,8},{8,9},{9,10},{10,1... | collective-permute-start | bytes 138248 | tf_op jit(solution)/shard_map/ppermute | solution.py:24
  253.3 1.2 collective-permute-done.14
  254.6 3.0 collective-permute-start.18
  257.7 1.9 collective-permute-start.19
  260.0 1.0 fusion.5
  261.0 1.7 collective-permute-done.19
  262.7 1.3 collective-permute-start.21
  264.0 4.6 %collective-permute-start.20 = (f32[4,6,1,128]{3,2,1,0:T(1,128)S(1)}, f32[4,6,1,128]{3,2,1,0:T(1,128)S(1)}, u32[]{:S(2)}, u32[]{:S(2)}) collective-permute-start(f32[4,6,1,128]{3,2,1,0:T(1,128)S(1)} %get-tuple-element.109), channel_id=1, source_target_pairs={{0,1},{1,2},{2,3},{3,4},{4,5},{5,6},{6,7},{7,8},{8,9},{9,10},{10,1... | collective-permute-start | bytes 36872 | tf_op jit(solution)/shard_map/ppermute | solution.py:24
  268.7 0.9 fusion.97
  269.6 3.4 collective-permute-start.16
  273.0 1.2 collective-permute-done.16
  274.3 0.3 scatter-add.26
  274.5 3.3 collective-permute-start.17
  278.0 1.0 collective-permute-done.17
  279.1 0.8 multiply_reduce_fusion
  279.9 68.6 %psum.31 = f32[]{:T(128)} all-reduce(f32[]{:T(128)} %get-tuple-element.99), channel_id=1, replica_groups=mesh['slab'=8,'tile'=16] {'slab','tile'}, use_global_device_ids=true, to_apply=%region_14.15 | all-reduce | flops 1 | bytes 8 | tf_op jit(solution)/shard_map/psum | solution.py:156
  349.7 0.7 multiply_subtract_fusion
  (111 shorter events, 5.1 us)
Async XLA Ops:
  0.6 0.7 copy-start.1
  1.9 0.7 copy-start.2
  5.5 11.5 %copy-start = (f32[12,256]{1,0:T(8,128)S(1)}, f32[12,256]{1,0:T(8,128)}, u32[]{:S(2)}) copy-start(f32[12,256]{1,0:T(8,128)} %param.20) | copy-start | bytes 36868
  5.5 11.5 %copy-start.3 = (f32[3,256]{1,0:T(4,128)S(1)}, f32[3,256]{1,0:T(4,128)}, u32[]{:S(2)}) copy-start(f32[3,256]{1,0:T(4,128)} %param.21) | copy-start | bytes 9220
  5.5 22.7 %all-to-all-start = ((s32[3,128,4]{2,0,1:T(4,128)}), s32[3,128,4]{2,0,1:T(4,128)S(1)}, u32[]{:S(2)}, u32[]{:S(2)}) async-start(s32[3,128,4]{2,0,1:T(4,128)} %copy.47), calls=%async_computation | async-start | bytes 524288 | tf_op jit(solution)/shard_map/all_to_all | solution.py:100
  28.3 15.5 %all-to-all-start.1 = ((f32[15,128,4]{0,2,1:T(4,128)}), f32[15,128,4]{0,2,1:T(4,128)S(1)}, u32[]{:S(2)}, u32[]{:S(2)}) async-start(f32[15,128,4]{0,2,1:T(4,128)} %bitcast.10), calls=%async_computation.1 | async-start | bytes 524288 | tf_op jit(solution)/shard_map/all_to_all | solution.py:99
  49.8 3.5 %collective-permute-start = (f32[3,10,3,128]{3,2,0,1:T(4,128)S(1)}, f32[3,10,3,128]{3,2,0,1:T(4,128)S(1)}, u32[]{:S(2)}, u32[]{:S(2)}) collective-permute-start(f32[3,10,3,128]{3,2,0,1:T(4,128)S(1)} %slice.693), channel_id=1, source_target_pairs={{0,1},{1,2},{2,3},{3,4},{4,5},{5,6},{6,7},{7,8},{8,9},{9,10},{10,1... | collective-permute-start | bytes 138248 | tf_op jit(solution)/shard_map/ppermute | solution.py:16
  53.6 4.9 %collective-permute-start.1 = (f32[3,3,8,128]{3,2,1,0:T(8,128)S(1)}, f32[3,3,8,128]{3,2,1,0:T(8,128)S(1)}, u32[]{:S(2)}, u32[]{:S(2)}) collective-permute-start(f32[3,3,8,128]{3,2,1,0:T(8,128)S(1)} %copy.72), channel_id=1, source_target_pairs={{0,16},{16,32},{32,48},{48,64},{64,80},{80,96},{96,112},{1,17},{17... | collective-permute-start | bytes 110600 | tf_op jit(solution)/shard_map/ppermute | solution.py:16
  58.8 7.5 %collective-permute-start.2 = (f32[3,3,8,128]{3,2,1,0:T(8,128)S(1)}, f32[3,3,8,128]{3,2,1,0:T(8,128)S(1)}, u32[]{:S(2)}, u32[]{:S(2)}) collective-permute-start(f32[3,3,8,128]{3,2,1,0:T(8,128)S(1)} %copy.74), channel_id=1, source_target_pairs={{0,16},{16,32},{32,48},{48,64},{64,80},{80,96},{96,112},{1,17},{17... | collective-permute-start | bytes 110600 | tf_op jit(solution)/shard_map/ppermute | solution.py:24
  64.3 5.3 %collective-permute-start.3 = (f32[3,3,8,128]{3,2,1,0:T(8,128)S(1)}, f32[3,3,8,128]{3,2,1,0:T(8,128)S(1)}, u32[]{:S(2)}, u32[]{:S(2)}) collective-permute-start(f32[3,3,8,128]{3,2,1,0:T(8,128)S(1)} %copy_add_fusion), channel_id=1, source_target_pairs={{16,0},{32,16},{48,32},{64,48},{80,64},{96,80},{112,96},{17,1},{33... | collective-permute-start | bytes 110600 | tf_op jit(solution)/shard_map/ppermute | solution.py:27
  69.7 6.0 %collective-permute-start.5 = (f32[3,10,3,128]{3,2,1,0:T(4,128)S(1)}, f32[3,10,3,128]{3,2,1,0:T(4,128)S(1)}, u32[]{:S(2)}, u32[]{:S(2)}) collective-permute-start(f32[3,10,3,128]{3,2,1,0:T(4,128)S(1)} %get-tuple-element.106), channel_id=1, source_target_pairs={{1,0},{2,1},{3,2},{4,3},{5,4},{6,5},{7,6},{8,7},{9,8},{10,9},{11,1... | collective-permute-start | bytes 138248 | tf_op jit(solution)/shard_map/ppermute | solution.py:27
  71.0 5.9 %collective-permute-start.4 = (f32[3,10,3,128]{3,2,1,0:T(4,128)S(1)}, f32[3,10,3,128]{3,2,1,0:T(4,128)S(1)}, u32[]{:S(2)}, u32[]{:S(2)}) collective-permute-start(f32[3,10,3,128]{3,2,1,0:T(4,128)S(1)} %get-tuple-element.107), channel_id=1, source_target_pairs={{0,1},{1,2},{2,3},{3,4},{4,5},{5,6},{6,7},{7,8},{8,9},{9,10},{10,1... | collective-permute-start | bytes 138248 | tf_op jit(solution)/shard_map/ppermute | solution.py:24
  77.0 6.3 %collective-permute-start.8 = (f32[4,1,8,128]{3,2,1,0:T(8,128)S(1)}, f32[4,1,8,128]{3,2,1,0:T(8,128)S(1)}, u32[]{:S(2)}, u32[]{:S(2)}) collective-permute-start(f32[4,1,8,128]{3,2,1,0:T(8,128)S(1)} %get-tuple-element.114), channel_id=1, source_target_pairs={{0,16},{16,32},{32,48},{48,64},{64,80},{80,96},{96,112},{1,17},{17... | collective-permute-start | bytes 49160 | tf_op jit(solution)/shard_map/ppermute | solution.py:24
  79.8 5.1 %collective-permute-start.9 = (f32[4,1,8,128]{3,2,1,0:T(8,128)S(1)}, f32[4,1,8,128]{3,2,1,0:T(8,128)S(1)}, u32[]{:S(2)}, u32[]{:S(2)}) collective-permute-start(f32[4,1,8,128]{3,2,1,0:T(8,128)S(1)} %get-tuple-element.115), channel_id=1, source_target_pairs={{16,0},{32,16},{48,32},{64,48},{80,64},{96,80},{112,96},{17,1},{33... | collective-permute-start | bytes 49160 | tf_op jit(solution)/shard_map/ppermute | solution.py:27
  84.9 10.5 %collective-permute-start.11 = (f32[4,6,1,128]{3,2,1,0:T(1,128)S(1)}, f32[4,6,1,128]{3,2,1,0:T(1,128)S(1)}, u32[]{:S(2)}, u32[]{:S(2)}) collective-permute-start(f32[4,6,1,128]{3,2,1,0:T(1,128)S(1)} %get-tuple-element.110), channel_id=1, source_target_pairs={{1,0},{2,1},{3,2},{4,3},{5,4},{6,5},{7,6},{8,7},{9,8},{10,9},{11,1... | collective-permute-start | bytes 36872 | tf_op jit(solution)/shard_map/ppermute | solution.py:27
  86.2 9.2 %collective-permute-start.10 = (f32[4,6,1,128]{3,2,1,0:T(1,128)S(1)}, f32[4,6,1,128]{3,2,1,0:T(1,128)S(1)}, u32[]{:S(2)}, u32[]{:S(2)}) collective-permute-start(f32[4,6,1,128]{3,2,1,0:T(1,128)S(1)} %get-tuple-element.111), channel_id=1, source_target_pairs={{0,1},{1,2},{2,3},{3,4},{4,5},{5,6},{6,7},{7,8},{8,9},{9,10},{10,1... | collective-permute-start | bytes 36872 | tf_op jit(solution)/shard_map/ppermute | solution.py:24
  91.7 4.9 %collective-permute-start.6 = (f32[3,10,3,128]{3,2,1,0:T(4,128)S(1)}, f32[3,10,3,128]{3,2,1,0:T(4,128)S(1)}, u32[]{:S(2)}, u32[]{:S(2)}) collective-permute-start(f32[3,10,3,128]{3,2,1,0:T(4,128)S(1)} %slice.701), channel_id=1, source_target_pairs={{0,1},{1,2},{2,3},{3,4},{4,5},{5,6},{6,7},{7,8},{8,9},{9,10},{10,1... | collective-permute-start | bytes 138248 | tf_op jit(solution)/shard_map/ppermute | solution.py:16
  97.0 4.3 %collective-permute-start.7 = (f32[3,3,8,128]{3,2,1,0:T(8,128)S(1)}, f32[3,3,8,128]{3,2,1,0:T(8,128)S(1)}, u32[]{:S(2)}, u32[]{:S(2)}) collective-permute-start(f32[3,3,8,128]{3,2,1,0:T(8,128)S(1)} %slice.703), channel_id=1, source_target_pairs={{0,16},{16,32},{32,48},{48,64},{64,80},{80,96},{96,112},{1,17},{17... | collective-permute-start | bytes 110600 | tf_op jit(solution)/shard_map/ppermute | solution.py:16
  238.9 5.5 %collective-permute-start.12 = (f32[3,3,8,128]{3,2,1,0:T(8,128)S(1)}, f32[3,3,8,128]{3,2,1,0:T(8,128)S(1)}, u32[]{:S(2)}, u32[]{:S(2)}) collective-permute-start(f32[3,3,8,128]{3,2,1,0:T(8,128)S(1)} %get-tuple-element.121), channel_id=1, source_target_pairs={{0,16},{16,32},{32,48},{48,64},{64,80},{80,96},{96,112},{1,17},{17... | collective-permute-start | bytes 110600 | tf_op jit(solution)/shard_map/ppermute | solution.py:24
  242.5 5.3 %collective-permute-start.13 = (f32[3,3,8,128]{3,2,1,0:T(8,128)S(1)}, f32[3,3,8,128]{3,2,1,0:T(8,128)S(1)}, u32[]{:S(2)}, u32[]{:S(2)}) collective-permute-start(f32[3,3,8,128]{3,2,1,0:T(8,128)S(1)} %get-tuple-element.122), channel_id=1, source_target_pairs={{16,0},{32,16},{48,32},{64,48},{80,64},{96,80},{112,96},{17,1},{33... | collective-permute-start | bytes 110600 | tf_op jit(solution)/shard_map/ppermute | solution.py:27
  247.9 5.4 %collective-permute-start.15 = (f32[3,10,3,128]{3,2,1,0:T(4,128)S(1)}, f32[3,10,3,128]{3,2,1,0:T(4,128)S(1)}, u32[]{:S(2)}, u32[]{:S(2)}) collective-permute-start(f32[3,10,3,128]{3,2,1,0:T(4,128)S(1)} %get-tuple-element.104), channel_id=1, source_target_pairs={{1,0},{2,1},{3,2},{4,3},{5,4},{6,5},{7,6},{8,7},{9,8},{10,9},{11,1... | collective-permute-start | bytes 138248 | tf_op jit(solution)/shard_map/ppermute | solution.py:27
  249.2 5.3 %collective-permute-start.14 = (f32[3,10,3,128]{3,2,1,0:T(4,128)S(1)}, f32[3,10,3,128]{3,2,1,0:T(4,128)S(1)}, u32[]{:S(2)}, u32[]{:S(2)}) collective-permute-start(f32[3,10,3,128]{3,2,1,0:T(4,128)S(1)} %get-tuple-element.105), channel_id=1, source_target_pairs={{0,1},{1,2},{2,3},{3,4},{4,5},{5,6},{6,7},{7,8},{8,9},{9,10},{10,1... | collective-permute-start | bytes 138248 | tf_op jit(solution)/shard_map/ppermute | solution.py:24
  254.6 6.3 %collective-permute-start.18 = (f32[4,1,8,128]{3,2,1,0:T(8,128)S(1)}, f32[4,1,8,128]{3,2,1,0:T(8,128)S(1)}, u32[]{:S(2)}, u32[]{:S(2)}) collective-permute-start(f32[4,1,8,128]{3,2,1,0:T(8,128)S(1)} %get-tuple-element.112), channel_id=1, source_target_pairs={{0,16},{16,32},{32,48},{48,64},{64,80},{80,96},{96,112},{1,17},{17... | collective-permute-start | bytes 49160 | tf_op jit(solution)/shard_map/ppermute | solution.py:24
  257.7 5.1 %collective-permute-start.19 = (f32[4,1,8,128]{3,2,1,0:T(8,128)S(1)}, f32[4,1,8,128]{3,2,1,0:T(8,128)S(1)}, u32[]{:S(2)}, u32[]{:S(2)}) collective-permute-start(f32[4,1,8,128]{3,2,1,0:T(8,128)S(1)} %get-tuple-element.113), channel_id=1, source_target_pairs={{16,0},{32,16},{48,32},{64,48},{80,64},{96,80},{112,96},{17,1},{33... | collective-permute-start | bytes 49160 | tf_op jit(solution)/shard_map/ppermute | solution.py:27
  262.7 10.2 %collective-permute-start.21 = (f32[4,6,1,128]{3,2,1,0:T(1,128)S(1)}, f32[4,6,1,128]{3,2,1,0:T(1,128)S(1)}, u32[]{:S(2)}, u32[]{:S(2)}) collective-permute-start(f32[4,6,1,128]{3,2,1,0:T(1,128)S(1)} %get-tuple-element.108), channel_id=1, source_target_pairs={{1,0},{2,1},{3,2},{4,3},{5,4},{6,5},{7,6},{8,7},{9,8},{10,9},{11,1... | collective-permute-start | bytes 36872 | tf_op jit(solution)/shard_map/ppermute | solution.py:27
  264.0 8.9 %collective-permute-start.20 = (f32[4,6,1,128]{3,2,1,0:T(1,128)S(1)}, f32[4,6,1,128]{3,2,1,0:T(1,128)S(1)}, u32[]{:S(2)}, u32[]{:S(2)}) collective-permute-start(f32[4,6,1,128]{3,2,1,0:T(1,128)S(1)} %get-tuple-element.109), channel_id=1, source_target_pairs={{0,1},{1,2},{2,3},{3,4},{4,5},{5,6},{6,7},{7,8},{8,9},{9,10},{10,1... | collective-permute-start | bytes 36872 | tf_op jit(solution)/shard_map/ppermute | solution.py:24
  269.6 4.6 %collective-permute-start.16 = (f32[3,10,3,128]{3,2,1,0:T(4,128)S(1)}, f32[3,10,3,128]{3,2,1,0:T(4,128)S(1)}, u32[]{:S(2)}, u32[]{:S(2)}) collective-permute-start(f32[3,10,3,128]{3,2,1,0:T(4,128)S(1)} %slice.720), channel_id=1, source_target_pairs={{0,1},{1,2},{2,3},{3,4},{4,5},{5,6},{6,7},{7,8},{8,9},{9,10},{10,1... | collective-permute-start | bytes 138248 | tf_op jit(solution)/shard_map/ppermute | solution.py:16
  274.5 4.4 %collective-permute-start.17 = (f32[3,3,8,128]{3,2,1,0:T(8,128)S(1)}, f32[3,3,8,128]{3,2,1,0:T(8,128)S(1)}, u32[]{:S(2)}, u32[]{:S(2)}) collective-permute-start(f32[3,3,8,128]{3,2,1,0:T(8,128)S(1)} %slice.722), channel_id=1, source_target_pairs={{0,16},{16,32},{32,48},{48,64},{64,80},{80,96},{96,112},{1,17},{17... | collective-permute-start | bytes 110600 | tf_op jit(solution)/shard_map/ppermute | solution.py:16
where the time goes:
time: 352 us; the launch traced here: 350 us
  blocking collectives  202 us (57%)
  starting transfers between devices  79.8 us (23%)
  waiting for transfers between devices  37.1 us (11%)
  local copies, waits for them, and re-layouts  14.3 us (4%)
  between operations  6.69 us (2%)
  other arithmetic  5.74 us (2%)
  matrix products  4.65 us (1%)
    psum x2, blocking collectives, squares(): return lax.psum(jnp.sum(residual * residual), ('slab', 'tile'))  133 us
    psum x1, blocking collectives, local(): alpha = norm_now / lax.psum(jnp.sum(direction * image), ('slab', 'tile'))  68.6 us
    ppermute x8, starting transfers between devices, extended(): lax.ppermute(lax.slice_in_dim(block, block.shape[dim] - width, None, axis...  31.4 us
    ppermute x6, starting transfers between devices, passed_along(): lax.ppermute(value, axis, [(source, source + steps) for source in range(i...  19.7 us
    ppermute x8, starting transfers between devices, extended(): lax.ppermute(lax.slice_in_dim(block, 0, width, axis=dim), axis, backward)  13 us
    all_to_all x1, starting transfers between devices, local(): lax.all_to_all(offsets_out, ('slab', 'tile'), split_axis=1, concat_axis=1...  11.5 us
    ppermute x8, waiting for transfers between devices, extended(): lax.ppermute(lax.slice_in_dim(block, 0, width, axis=dim), axis, backward)  9.96 us
    all_to_all x1, waiting for transfers between devices, local(): lax.all_to_all(offsets_out, ('slab', 'tile'), split_axis=1, concat_axis=1...  9.28 us
  transfers between devices with their start and end apart: 24, of which 14 were waited for; matrix products, arithmetic and copies ran while one was open for 3% of the time, Pallas kernels for 0%

commit v1 on v0

v1 whole, which is shorter than its diff:
```python
import functools

import jax
import jax.numpy as jnp
from jax import lax
from jax.experimental import pallas as pl
from jax.experimental.pallas import tpu as pltpu
from jax.sharding import PartitionSpec as P

CZ = 4
CX = 8
NY = 128
CAP = 4
LANES = 128
F32 = jnp.float32
BF16 = jnp.bfloat16
NT = (((1,), (1,)), ((), ()))
NN = (((1,), (0,)), ((), ()))
HALO = (
    ((-1, -1), (0, 3), (0, 3), 4, 8),
    ((0, -1), (0, 4), (0, 3), 0, 8),
    ((0, 1), (0, 4), (6, 2), 0, 14),
    ((-1, 0), (0, 3), (0, 8), 4, 0),
    ((1, 0), (2, 2), (0, 8), 7, 0),
    ((1, 1), (3, 1), (7, 1), 8, 15),
    ((1, -1), (3, 1), (0, 1), 8, 8),
    ((-1, 1), (0, 1), (7, 1), 4, 15),
)
SPILL = (
    ((1, 1), (4, 3), (8, 3)),
    ((0, 1), (0, 4), (8, 3)),
    ((1, 0), (4, 3), (0, 8)),
)


def split(value):
    high = value.astype(BF16)
    return high, (value - high.astype(F32)).astype(BF16)


def product(left, right, dims):
    dot = functools.partial(lax.dot_general, dimension_numbers=dims, preferred_element_type=F32)
    return dot(left[0], right[0]) + (dot(left[0], right[1]) + dot(left[1], right[0]))


def kernel(
    slabs, tiles, owner_ref, base_ref, spline_ref, measured_ref, div_ref, bend_ref,
    solution_ref, residual_ref,
    pay, out_rows, by_slab, turned, by_tile,
    partial, spill, field, bent, source, sum_slab, sum_tile,
    pass_send, pass_slab_recv, pass_tile_recv, spill_send, spill_recv, halo_send, halo_recv,
    sum_send, sum_slab_recv, sum_tile_recv,
):
    devices = slabs * tiles
    slab, tile = lax.axis_index("slab"), lax.axis_index("tile")
    count = owner_ref.shape[1]

    barrier = pltpu.get_barrier_semaphore()

    def mesh_at(s, t):
        return {"slab": s, "tile": t}

    def other_slab(step):
        return lax.rem(slab + step, slabs)

    def other_tile(step):
        return lax.rem(tile + step, tiles)

    field[...] = jnp.zeros_like(field)
    spill[...] = jnp.zeros_like(spill)

    for step in range(1, slabs):
        pl.semaphore_signal(barrier, inc=1, device_id=mesh_at(other_slab(step), tile))
    for step in range(1, tiles):
        pl.semaphore_signal(barrier, inc=1, device_id=mesh_at(slab, other_tile(step)))
    for s in (1, slabs - 1):
        for t in (1, tiles - 1):
            pl.semaphore_signal(barrier, inc=1, device_id=mesh_at(other_slab(s), other_tile(t)))

    pay[...] = jnp.zeros_like(pay)
    pay[0:12, :] = spline_ref[...]
    pay[12:15, :] = measured_ref[...]
    pay[15:18, :] = base_ref[...].astype(F32)
    owner = owner_ref[...]
    onehot = (lax.broadcasted_iota(jnp.int32, (devices, count), 0) == owner).astype(F32)
    onehot_b = onehot.astype(BF16)
    earlier = (
        lax.broadcasted_iota(jnp.int32, (count, count), 0)
        < lax.broadcasted_iota(jnp.int32, (count, count), 1)
    ).astype(BF16)
    before = lax.dot_general(onehot_b, earlier, NN, preferred_element_type=F32)
    rank = jnp.sum(onehot * before, axis=0, keepdims=True)
    payload = pay[...]
    slots = jnp.concatenate([jnp.where(rank == k, payload, 0.0) for k in range(CAP)], axis=0)
    high, low = split(slots)
    lowest = (slots - high.astype(F32) - low.astype(F32)).astype(BF16)
    rows = [lax.dot_general(onehot_b, part, NT, preferred_element_type=F32) for part in (high, low, lowest)]
    out_rows[...] = ((rows[0] + rows[1]) + rows[2]).reshape(slabs, tiles, LANES)

    pl.semaphore_wait(barrier, slabs - 1 + tiles - 1 + 4)

    sends = []
    for step in range(1, slabs):
        to = other_slab(step)
        copy = pltpu.make_async_remote_copy(
            src_ref=out_rows.at[to], dst_ref=by_slab.at[slab],
            send_sem=pass_send.at[step], recv_sem=pass_slab_recv.at[slab],
            device_id=mesh_at(to, tile),
        )
        copy.start()
        sends.append(copy)
    by_slab[slab] = out_rows[slab]
    for step in range(1, slabs):
        origin = other_slab(step)
        pltpu.make_async_remote_copy(
            src_ref=out_rows.at[origin], dst_ref=by_slab.at[origin],
            send_sem=pass_send.at[step], recv_sem=pass_slab_recv.at[origin],
            device_id=mesh_at(origin, tile),
        ).wait_recv()
    for s in range(slabs):
        turned[pl.ds(s, tiles, stride=slabs), :] = by_slab[s]
    for step in range(1, tiles):
        to = other_tile(step)
        copy = pltpu.make_async_remote_copy(
            src_ref=turned.at[pl.ds(to * slabs, slabs)], dst_ref=by_tile.at[pl.ds(tile * slabs, slabs)],
            send_sem=pass_send.at[slabs + step], recv_sem=pass_tile_recv.at[tile],
            device_id=mesh_at(slab, to),
        )
        copy.start()
        sends.append(copy)
    by_tile[pl.ds(tile * slabs, slabs), :] = turned[pl.ds(tile * slabs, slabs), :]
    for step in range(1, tiles):
        origin = other_tile(step)
        pltpu.make_async_remote_copy(
            src_ref=turned.at[pl.ds(origin * slabs, slabs)], dst_ref=by_tile.at[pl.ds(origin * slabs, slabs)],
            send_sem=pass_send.at[slabs + step], recv_sem=pass_tile_recv.at[origin],
            device_id=mesh_at(slab, origin),
        ).wait_recv()

    lanes_first = by_tile[...].T
    owned = jnp.concatenate([lanes_first[32 * k : 32 * k + 32] for k in range(CAP)], axis=1)
    total = owned.shape[1]

    def spread_weights(cells, base, first):
        offset = lax.broadcasted_iota(jnp.int32, (cells, total), 0).astype(F32) - owned[base : base + 1]
        result = jnp.zeros((cells, total), F32)
        for step in range(4):
            result = jnp.where(offset == float(step), owned[first + step : first + step + 1], result)
        return result

    weight_z = spread_weights(8, 15, 0)
    weight_x = spread_weights(16, 16, 4)
    weight_y = spread_weights(NY, 17, 8)
    plane = jnp.concatenate([weight_z[z : z + 1] * weight_x for z in range(CZ + 3)], axis=0)
    plane_parts = split(plane)

    def send_spread(turn, values):
        sends = []
        columns = split(jnp.concatenate([weight_y * values[c] for c in range(3)], axis=0))
        partial[turn] = product(plane_parts, columns, NT).reshape(CZ + 3, 16, 3 * NY)
        for number, ((s, t), z, x) in enumerate(SPILL):
            copy = spill_copy(turn, number)

            @pl.when(exists(s, t))
            def _():
                copy.start()

    def exists(s, t):
        inside = None
        if s:
            inside = (slab < slabs - 1) if s > 0 else (slab > 0)
        if t:
            along = (tile < tiles - 1) if t > 0 else (tile > 0)
            inside = along if inside is None else jnp.logical_and(inside, along)
        return inside

    def toward(s, t):
        return mesh_at(lax.rem(slab + s + slabs, slabs), lax.rem(tile + t + tiles, tiles))

    def spill_copy(turn, number):
        (s, t), (z, zs), (x, xs) = SPILL[number]
        return pltpu.make_async_remote_copy(
            src_ref=partial.at[turn, pl.ds(z, zs), pl.ds(x, xs)],
            dst_ref=spill.at[turn, number, pl.ds(0, zs), pl.ds(0, xs)],
            send_sem=spill_send.at[turn, number], recv_sem=spill_recv.at[turn, number],
            device_id=toward(s, t),
        )

    def gather_spread(turn):
        for number, ((s, t), z, x) in enumerate(SPILL):

            @pl.when(exists(-s, -t))
            def _():
                spill_copy(turn, number).wait_recv()

        result = []
        for z in range(CZ):
            value = partial[turn, z, 0:CX] + spill[turn, 1, z]
            if z < 3:
                value = value + (spill[turn, 0, z] + spill[turn, 2, z])
            result.append(value)
        return result

    def halo_copy(turn, number):
        (s, t), (z, zs), (x, xs), to_z, to_x = HALO[number]
        return pltpu.make_async_remote_copy(
            src_ref=field.at[turn, pl.ds(z, zs), pl.ds(x, xs)],
            dst_ref=field.at[turn, pl.ds(to_z, zs), pl.ds(to_x, xs)],
            send_sem=halo_send.at[turn, number], recv_sem=halo_recv.at[turn, number],
            device_id=toward(s, t),
        )

    def send_halo(turn):
        for number, entry in enumerate(HALO):
            copy = halo_copy(turn, number)

            @pl.when(exists(*entry[0]))
            def _():
                copy.start()

    def wait_halo(turn):
        for number, entry in enumerate(HALO):

            @pl.when(exists(-entry[0][0], -entry[0][1]))
            def _():
                halo_copy(turn, number).wait_recv()

    def read_samples(turn):
        readings = []
        for c in range(3):
            part = field[turn, 0 : CZ + 3, :, c * NY : (c + 1) * NY].reshape((CZ + 3) * 16, NY).T
            seen = product(split(part), plane_parts, NN)
            readings.append(jnp.sum(seen * weight_y, axis=0, keepdims=True))
        return readings

    lane = lax.broadcasted_iota(jnp.int32, (16, NY), 1)
    place = lax.broadcasted_iota(jnp.int32, (16, NY), 0)
    has_low_z, has_high_z = slab > 0, slab < slabs - 1
    inside_x = (place < CX) | ((place == CX) & (tile < tiles - 1)) | ((place == 15) & (tile > 0))

    def after_y(value):
        return jnp.where(lane == NY - 1, 0.0, pltpu.roll(value, NY - 1, 1))

    def before_y(value):
        return jnp.where(lane == 0, 0.0, pltpu.roll(value, 1, 1))

    def after_x(value):
        return pltpu.roll(value, 15, 0)

    def before_x(value):
        return pltpu.roll(value, 1, 0)

    def around(below, middle, above):
        total = (above + below) + (after_x(middle) + before_x(middle))
        return total + (after_y(middle) + before_y(middle)) - 6.0 * middle

    def cell(turn, c, z):
        return field[turn, z if z >= 0 else z + 9, :, c * NY : (c + 1) * NY]

    def inside(value, z):
        keep = inside_x
        if z < 0:
            keep = keep & has_low_z
        if z >= CZ:
            keep = keep & has_high_z
        return jnp.where(keep, value, 0.0)

    def smooth(turn):
        for c in range(3):
            for z in range(-1, CZ + 1):
                value = around(cell(turn, c, z - 1), cell(turn, c, z), cell(turn, c, z + 1))
                bent[turn, c, z + 1] = inside(value, z)
        for z in range(-1, CZ):
            along_z = cell(turn, 0, z + 1) - cell(turn, 0, z)
            along_x = after_x(cell(turn, 1, z)) - cell(turn, 1, z)
            along_y = after_y(cell(turn, 2, z)) - cell(turn, 2, z)
            source[turn, z + 1] = inside(along_z + along_x + along_y, z)

    div_weight = div_ref[0]
    bend_weight = bend_ref[0]

    def penalties(turn, c, z):
        here = source[turn, z + 1]
        if c == 0:
            pushed = source[turn, z] - here
        elif c == 1:
            pushed = before_x(here) - here
        else:
            pushed = before_y(here) - here
        again = around(bent[turn, c, z], bent[turn, c, z + 1], bent[turn, c, z + 2])
        return (div_weight * pushed + bend_weight * again)[0:CX]

    def all_penalties(turn):
        return [
            jnp.concatenate([penalties(turn, c, z) for c in range(3)], axis=1) for z in range(CZ)
        ]

    def one(value):
        return jnp.sum(jnp.sum(value, axis=0, keepdims=True), axis=1, keepdims=True)

    row_lane = lax.broadcasted_iota(jnp.int32, (1, LANES), 1)

    def sum_copy(turn, stage, step, incoming):
        buffer, size, mine, peer = (
            (sum_slab, slabs, slab, other_slab(step)) if stage == 0 else (sum_tile, tiles, tile, other_tile(step))
        )
        received = sum_slab_recv if stage == 0 else sum_tile_recv
        where = peer if incoming else mine
        return pltpu.make_async_remote_copy(
            src_ref=buffer.at[turn, pl.ds(mine, 1)], dst_ref=buffer.at[turn, pl.ds(where, 1)],
            send_sem=sum_send.at[turn, stage, step], recv_sem=received.at[turn, where],
            device_id=mesh_at(peer, tile) if stage == 0 else mesh_at(slab, peer),
        )

    def start_sum(turn, values):
        row = jnp.zeros((1, LANES), F32)
        for number, value in enumerate(values):
            row = jnp.where(row_lane == number, value, row)
        sum_slab[turn, pl.ds(slab, 1)] = row
        for step in range(1, slabs):
            sum_copy(turn, 0, step, False).start()

    def turn_sum(turn):
        for step in range(1, slabs):
            sum_copy(turn, 0, step, True).wait_recv()
        sum_tile[turn, pl.ds(tile, 1)] = jnp.sum(sum_slab[turn], axis=0, keepdims=True)
        for step in range(1, tiles):
            sum_copy(turn, 1, step, False).start()

    def end_sum(turn, number):
        for step in range(1, tiles):
            sum_copy(turn, 1, step, True).wait_recv()
        row = jnp.sum(sum_tile[turn], axis=0, keepdims=True)
        return [row[:, i : i + 1] for i in range(number)]

    send_spread(0, [owned[12 + c : 13 + c] for c in range(3)])
    start = gather_spread(0)
    for z in range(CZ):
        field[0, z, 0:CX] = start[z]
    send_halo(0)
    square = one(functools.reduce(jnp.add, [v * v for v in start]))

    wait_halo(0)
    read_start = read_samples(0)
    send_spread(1, read_start)
    smooth(0)

    def energy(readings, sources, bends):
        seen = one(functools.reduce(jnp.add, [v * v for v in readings]))
        pushed = one(functools.reduce(jnp.add, [v * v for v in sources]))
        again = one(functools.reduce(jnp.add, [v * v for v in bends]))
        return seen + div_weight * pushed + bend_weight * again

    def own_source(turn):
        return [source[turn, z + 1, 0:CX] for z in range(CZ)]

    def own_bent(turn):
        return [bent[turn, c, z + 1, 0:CX] for c in range(3) for z in range(CZ)]

    start_sum(0, [square, energy(read_start, own_source(0), own_bent(0))])
    held = all_penalties(0)
    turn_sum(0)
    image = [v + p for v, p in zip(gather_spread(1), held)]
    for z in range(CZ):
        field[1, z, 0:CX] = image[z]
    send_halo(1)
    norm, curvature = end_sum(0, 2)
    step_size = norm / curvature
    left = [b - step_size * y for b, y in zip(start, image)]
    left_square = one(functools.reduce(jnp.add, [v * v for v in left]))
    left_image = one(functools.reduce(jnp.add, [v * y for v, y in zip(left, image)]))

    wait_halo(1)
    read_image = read_samples(1)
    smooth(1)
    left_energy = energy(
        [a - step_size * b for a, b in zip(read_start, read_image)],
        [a - step_size * b for a, b in zip(own_source(0), own_source(1))],
        [a - step_size * b for a, b in zip(own_bent(0), own_bent(1))],
    )
    start_sum(1, [left_square, left_image, left_energy])
    send_spread(2, read_image)
    held = all_penalties(1)
    turn_sum(1)
    second = [v + p for v, p in zip(gather_spread(2), held)]
    left_square, left_image, left_energy = end_sum(1, 3)

    ratio = left_square / norm
    bowed = left_energy + 2.0 * ratio * left_image + ratio * ratio * curvature
    step_next = left_square / bowed
    for z in range(CZ):
        direction = left[z] + ratio * start[z]
        pushed = (image[z] - step_size * second[z]) + ratio * image[z]
        answer = step_size * start[z] + step_next * direction
        rest = left[z] - step_next * pushed
        for c in range(3):
            solution_ref[c, z] = answer[:, c * NY : (c + 1) * NY]
            residual_ref[c, z] = rest[:, c * NY : (c + 1) * NY]

    for copy in sends:
        copy.wait_send()
    for turn in range(3):
        for number, ((s, t), z, x) in enumerate(SPILL):

            @pl.when(exists(s, t))
            def _():
                spill_copy(turn, number).wait_send()

    for turn in range(2):
        for number, entry in enumerate(HALO):

            @pl.when(exists(*entry[0]))
            def _():
                halo_copy(turn, number).wait_send()

        for step in range(1, slabs):
            sum_copy(turn, 0, step, False).wait_send()
        for step in range(1, tiles):
            sum_copy(turn, 1, step, False).wait_send()


def local(slabs, tiles, owner, block_base, spline_weights, measured, div_weight, bend_weight):
    devices = slabs * tiles
    count = owner.shape[0]
    vmem = pl.BlockSpec(memory_space=pltpu.VMEM)
    smem = pl.BlockSpec(memory_space=pltpu.SMEM)
    dma = pltpu.SemaphoreType.DMA
    wide = 3 * NY
    out = jax.ShapeDtypeStruct((3, CZ, CX, NY), F32)
    return pl.pallas_call(
        functools.partial(kernel, slabs, tiles),
        out_shape=(out, out),
        in_specs=[vmem] * 4 + [smem] * 2,
        out_specs=(vmem, vmem),
        scratch_shapes=[
            pltpu.VMEM((32, count), F32),
            pltpu.VMEM((slabs, tiles, LANES), F32),
            pltpu.VMEM((slabs, tiles, LANES), F32),
            pltpu.VMEM((devices, LANES), F32),
            pltpu.VMEM((devices, LANES), F32),
            pltpu.VMEM((3, CZ + 3, 16, wide), F32),
            pltpu.VMEM((3, 3, CZ, CX, wide), F32),
            pltpu.VMEM((2, 9, 16, wide), F32),
            pltpu.VMEM((2, 3, CZ + 2, 16, NY), F32),
            pltpu.VMEM((2, CZ + 1, 16, NY), F32),
            pltpu.VMEM((2, slabs, LANES), F32),
            pltpu.VMEM((2, tiles, LANES), F32),
            dma((slabs + tiles,)),
            dma((slabs,)),
            dma((tiles,)),
            dma((3, 3)),
            dma((3, 3)),
            dma((2, 8)),
            dma((2, 8)),
            dma((2, 2, max(slabs, tiles))),
            dma((2, slabs)),
            dma((2, tiles)),
        ],
        compiler_params=pltpu.CompilerParams(collective_id=0, has_side_effects=True),
    )(owner.reshape(1, count), block_base, spline_weights, measured, div_weight, bend_weight)


def solution(mesh):
    placed = (
        P(("slab", "tile"), None),
        P(None, ("slab", "tile")),
        P(None, ("slab", "tile")),
        P(None, ("slab", "tile")),
        P(),
        P(),
    )
    sizes = dict(zip(mesh.axis_names, mesh.devices.shape))
    return jax.shard_map(
        functools.partial(local, sizes["slab"], sizes["tile"]),
        mesh=mesh,
        in_specs=placed,
        out_specs=(P(None, "slab", "tile", None), P(None, "slab", "tile", None)),
        check_vma=False,
    )
```

time: 352 us -> 50.6 us (0.14)
  blocking collectives: 202 us -> 0 us
  starting transfers between devices: 79.8 us -> 0 us
  Pallas kernels: 0 us -> 46.2 us
  waiting for transfers between devices: 37.1 us -> 0 us
  local copies, waits for them, and re-layouts: 14.3 us -> 2.06 us
  other arithmetic: 5.74 us -> 0 us
  between operations: 6.69 us -> 1.94 us
  matrix products: 4.65 us -> 0 us
    psum x3 -> x0, blocking collectives: 202 us -> none  [the longest x2 133 us: squares(): return lax.psum(jnp.sum(residual * residual), ('slab', 'tile'))]
    ppermute x22 -> x0, starting transfers between devices: 64.2 us -> none  [the longest x8 31.4 us: extended(): lax.ppermute(lax.slice_in_dim(block, block.shape[dim] - width, None, axis...]
    pallas_call x0 -> x1, Pallas kernels: none -> 46.2 us  [local(): pl.pallas_call(functools.partial(kernel, slabs, tiles), out_shape=(out, o...]
    ppermute x22 -> x0, waiting for transfers between devices: 19.1 us -> none  [the longest x8 9.96 us: extended(): lax.ppermute(lax.slice_in_dim(block, 0, width, axis=dim), axis, backward)]
    all_to_all x2 -> x0, waiting for transfers between devices: 17.9 us -> none  [the longest x1 9.28 us: local(): lax.all_to_all(offsets_out, ('slab', 'tile'), split_axis=1, concat_axis=1...]
    all_to_all x2 -> x0, starting transfers between devices: 15.7 us -> none  [the longest x1 11.5 us: local(): lax.all_to_all(offsets_out, ('slab', 'tile'), split_axis=1, concat_axis=1...]
    slice x16 -> x0, local copies, waits for them, and re-layouts: 3.79 us -> none  [the longest x1 3.21 us: placed(): weights[step][:, None]]
  transfers between devices with their start and end apart: 24 -> 0, of which waited for: 14 -> 0; matrix products, arithmetic and copies ran while one was open for 3% -> 0% of each run, Pallas kernels for 0% -> 0%
where the time goes in v1:
time: 50.6 us; the launch traced here: 50.2 us
  Pallas kernels  46.2 us (91%)
  local copies, waits for them, and re-layouts  2.06 us (4%)
  between operations  1.94 us (4%)
    pallas_call x1, Pallas kernels, local(): pl.pallas_call(functools.partial(kernel, slabs, tiles), out_shape=(out, o...  46.2 us
    unnamed x4, local copies, waits for them, and re-layouts  2.06 us

profile of v1, /device:TPU:1, one launch (start us, length us, event | category | flops | bytes accessed | tf_op | source)
XLA Modules:
  0.0 50.2 jit_solution(11281865443213542185)
XLA Ops:
  1.9 46.2 %shard_map.77 = (f32[3,4,8,128]{3,2,1,0:T(8,128)}, f32[3,4,8,128]{3,2,1,0:T(8,128)}) custom-call(s32[1,256]{1,0:T(1,128)} %bitcast.1, s32[3,256]{1,0:T(4,128)} %base_ref.1, f32[12,256]{1,0:T(8,128)} %spline_ref.1, f32[3,256]{1,0:T(4,128)} %measured_ref.1, f32[1]{0:T(128)S(6)} %copy.10.div_ref, f32[1]{0:T(128)S(6)} %copy.11.bend_ref), custom_call_target="tpu_custom_call" | custom-call | tf_op jit(solution)/shard_map/pallas_call | solution.py:430
  48.1 0.0 copy-start
  48.1 1.4 %copy.12 = f32[3,4,8,128]{3,2,1,0:T(8,128)} copy(f32[3,4,8,128]{3,2,1,0:T(8,128)} %get-tuple-element.4) | data formatting | bytes 98304
  49.6 0.0 copy-done
  49.6 0.6 %copy.13 = f32[3,4,8,128]{3,2,1,0:T(8,128)} copy(f32[3,4,8,128]{3,2,1,0:T(8,128)S(1)} %copy-done) | data formatting | bytes 98304
Async XLA Ops:
  48.1 1.4 %copy-start = (f32[3,4,8,128]{3,2,1,0:T(8,128)S(1)}, f32[3,4,8,128]{3,2,1,0:T(8,128)}, u32[]{:S(2)}) copy-start(f32[3,4,8,128]{3,2,1,0:T(8,128)} %get-tuple-element.5) | copy-start | bytes 147460

commit v2 on v1

v2 whole, which is shorter than its diff:
```python
import functools

import jax
import jax.numpy as jnp
from jax import lax
from jax.experimental import pallas as pl
from jax.experimental.pallas import tpu as pltpu
from jax.sharding import PartitionSpec as P

CZ = 4
CX = 8
NY = 128
CAP = 4
LANES = 128
F32 = jnp.float32
BF16 = jnp.bfloat16
NT = (((1,), (1,)), ((), ()))
NN = (((1,), (0,)), ((), ()))
WIDE = (
    ((2, 1), (6, 1), (8, 3)),
    ((1, 1), (2, 5), (6, 5)),
    ((-1, -1), (0, 3), (0, 3)),
    ((1, -1), (3, 4), (0, 3)),
    ((-1, 1), (0, 3), (7, 4)),
    ((0, 1), (0, 7), (6, 5)),
    ((0, -1), (0, 7), (0, 3)),
    ((2, 0), (6, 1), (0, 6)),
    ((2, 0), (6, 1), (6, 2)),
    ((1, 0), (2, 5), (0, 6)),
    ((1, 0), (2, 5), (6, 5)),
    ((-1, 0), (0, 3), (0, 6)),
    ((-1, 0), (0, 3), (6, 5)),
)
LAST = (
    ((1, 1), (4, 3), (8, 3)),
    ((0, 1), (0, 4), (8, 3)),
    ((1, 0), (4, 3), (0, 6)),
    ((1, 0), (4, 3), (6, 2)),
)
ROUNDS = (WIDE, WIDE, LAST)


def landing(entry):
    (s, t), (z, _), (x, _) = entry
    row = x - CX * t + 2
    return z - CZ * s + 2, row % 8, row // 8


def split(value):
    high = value.astype(BF16)
    return high, (value - high.astype(F32)).astype(BF16)


def product(left, right, dims):
    dot = functools.partial(lax.dot_general, dimension_numbers=dims, preferred_element_type=F32)
    return dot(left[0], right[0]) + (dot(left[0], right[1]) + dot(left[1], right[0]))


def kernel(
    slabs, tiles, owner_in, base_in, spline_in, measured_in, div_in, bend_in,
    solution_ref, residual_ref,
    owner_ref, base_ref, spline_ref, measured_ref, div_ref, bend_ref, load_sem,
    pay, out_rows, by_slab, turned, by_tile,
    partial, field, bent, source, sum_slab, sum_tile,
    pass_send, pass_slab_recv, pass_tile_recv, wide_send, wide_recv,
    sum_send, sum_slab_recv, sum_tile_recv,
    *landed,
):
    landed = (landed[: len(WIDE)], landed[len(WIDE) : 2 * len(WIDE)], landed[2 * len(WIDE) :])
    devices = slabs * tiles
    slab, tile = lax.axis_index("slab"), lax.axis_index("tile")
    count = owner_ref.shape[1]

    barrier = pltpu.get_barrier_semaphore()
    drains = []

    def finish():
        for drain in drains:
            drain()

    def mesh_at(s, t):
        return {"slab": s, "tile": t}

    def other_slab(step):
        return lax.rem(slab + step, slabs)

    def other_tile(step):
        return lax.rem(tile + step, tiles)

    loads = [
        pltpu.make_async_copy(source, target, load_sem.at[number])
        for number, (source, target) in enumerate((
            (owner_in, owner_ref), (base_in, base_ref), (spline_in, spline_ref),
            (measured_in, measured_ref), (div_in, div_ref), (bend_in, bend_ref),
        ))
    ]
    for load in loads:
        load.start()

    for step in range(1, slabs):
        pl.semaphore_signal(barrier, inc=1, device_id=mesh_at(other_slab(step), tile))
    for step in range(1, tiles):
        pl.semaphore_signal(barrier, inc=1, device_id=mesh_at(slab, other_tile(step)))

    for buffers in landed:
        for buffer in buffers:
            buffer[...] = jnp.zeros_like(buffer)

    for load in loads:
        load.wait()

    pay[...] = jnp.zeros_like(pay)
    pay[0:12, :] = spline_ref[...]
    pay[12:15, :] = measured_ref[...]
    pay[15:18, :] = base_ref[...].astype(F32)
    owner = owner_ref[...]
    onehot = (lax.broadcasted_iota(jnp.int32, (devices, count), 0) == owner).astype(F32)
    onehot_b = onehot.astype(BF16)
    earlier = (
        lax.broadcasted_iota(jnp.int32, (count, count), 0)
        < lax.broadcasted_iota(jnp.int32, (count, count), 1)
    ).astype(BF16)
    before = lax.dot_general(onehot_b, earlier, NN, preferred_element_type=F32)
    rank = jnp.sum(onehot * before, axis=0, keepdims=True)
    payload = pay[...]
    slots = jnp.concatenate([jnp.where(rank == k, payload, 0.0) for k in range(CAP)], axis=0)
    high, low = split(slots)
    lowest = (slots - high.astype(F32) - low.astype(F32)).astype(BF16)
    rows = [lax.dot_general(onehot_b, part, NT, preferred_element_type=F32) for part in (high, low, lowest)]
    out_rows[...] = ((rows[0] + rows[1]) + rows[2]).reshape(slabs, tiles, LANES)

    pl.semaphore_wait(barrier, slabs - 1 + tiles - 1)

    for step in range(1, slabs):
        to = other_slab(step)
        copy = pltpu.make_async_remote_copy(
            src_ref=out_rows.at[to], dst_ref=by_slab.at[slab],
            send_sem=pass_send.at[step], recv_sem=pass_slab_recv.at[slab],
            device_id=mesh_at(to, tile),
        )
        copy.start()
        drains.append(copy.wait_send)
    by_slab[slab] = out_rows[slab]
    for step in range(1, slabs):
        origin = other_slab(step)
        pltpu.make_async_remote_copy(
            src_ref=out_rows.at[origin], dst_ref=by_slab.at[origin],
            send_sem=pass_send.at[step], recv_sem=pass_slab_recv.at[origin],
            device_id=mesh_at(origin, tile),
        ).wait_recv()
    for s in range(slabs):
        turned[pl.ds(s, tiles, stride=slabs), :] = by_slab[s]
    for step in range(1, tiles):
        to = other_tile(step)
        copy = pltpu.make_async_remote_copy(
            src_ref=turned.at[pl.ds(to * slabs, slabs)], dst_ref=by_tile.at[pl.ds(tile * slabs, slabs)],
            send_sem=pass_send.at[slabs + step], recv_sem=pass_tile_recv.at[tile],
            device_id=mesh_at(slab, to),
        )
        copy.start()
        drains.append(copy.wait_send)
    by_tile[pl.ds(tile * slabs, slabs), :] = turned[pl.ds(tile * slabs, slabs), :]
    for step in range(1, tiles):
        origin = other_tile(step)
        pltpu.make_async_remote_copy(
            src_ref=turned.at[pl.ds(origin * slabs, slabs)], dst_ref=by_tile.at[pl.ds(origin * slabs, slabs)],
            send_sem=pass_send.at[slabs + step], recv_sem=pass_tile_recv.at[origin],
            device_id=mesh_at(slab, origin),
        ).wait_recv()

    lanes_first = by_tile[...].T
    owned = jnp.concatenate([lanes_first[32 * k : 32 * k + 32] for k in range(CAP)], axis=1)
    total = owned.shape[1]

    def spread_weights(cells, base, first, shift=0):
        offset = lax.broadcasted_iota(jnp.int32, (cells, total), 0).astype(F32) - (owned[base : base + 1] + float(shift))
        result = jnp.zeros((cells, total), F32)
        for step in range(4):
            result = jnp.where(offset == float(step), owned[first + step : first + step + 1], result)
        return result

    weight_z = spread_weights(8, 15, 0)
    weight_x = spread_weights(16, 16, 4, 2)
    weight_y = spread_weights(NY, 17, 8)
    plane = jnp.concatenate([weight_z[z : z + 1] * weight_x for z in range(CZ + 3)], axis=0)
    plane_parts = split(plane)

    def spread(values):
        columns = split(jnp.concatenate([weight_y * values[c] for c in range(3)], axis=0))
        return product(plane_parts, columns, NT).reshape(CZ + 3, 16, 3 * NY)

    def exists(s, t):
        inside = None
        if s:
            inside = (slab < slabs - s) if s > 0 else (slab >= -s)
        if t:
            along = (tile < tiles - t) if t > 0 else (tile >= -t)
            inside = along if inside is None else jnp.logical_and(inside, along)
        return inside

    def wide_copy(turn, number):
        entry = ROUNDS[turn][number]
        (s, t), (z, zs), (x, xs) = entry
        _, row, _ = landing(entry)
        return pltpu.make_async_remote_copy(
            src_ref=partial.at[turn, pl.ds(z, zs), pl.ds(x + 2, xs)],
            dst_ref=landed[turn][number].at[pl.ds(0, zs), pl.ds(row, xs)],
            send_sem=wide_send.at[turn, number], recv_sem=wide_recv.at[turn, number],
            device_id=mesh_at(lax.rem(slab + s + slabs, slabs), lax.rem(tile + t + tiles, tiles)),
        )

    def send_wide(turn):
        for number, entry in enumerate(ROUNDS[turn]):
            start_to(*entry[0], wide_copy(turn, number))

    def start_to(s, t, copy):
        @pl.when(exists(s, t))
        def _():
            copy.start()

        def drain():
            @pl.when(exists(s, t))
            def _():
                copy.wait_send()

        drains.append(drain)

    def wait_wide(turn):
        for number, entry in enumerate(ROUNDS[turn]):

            @pl.when(exists(-entry[0][0], -entry[0][1]))
            def _():
                wide_copy(turn, number).wait_recv()

    def added_up(turn, z):
        halves = [None, None]

        def add(half, value):
            halves[half] = value if halves[half] is None else halves[half] + value

        for number, entry in enumerate(ROUNDS[turn]):
            first, _, half = landing(entry)
            if first <= z < first + entry[1][1]:
                add(half, landed[turn][number][z - first])
        if z >= 2:
            add(0, partial[turn, z - 2, 0:8])
            add(1, partial[turn, z - 2, 8:16])
        return jnp.concatenate(halves, axis=0)

    def in_grid(value, z):
        keep = high_x if z < CZ else high_x & has_high_z
        return jnp.where(keep, value, 0.0)

    def read_samples(turn):
        readings = []
        for c in range(3):
            part = field[turn, 2 : CZ + 5, :, c * NY : (c + 1) * NY].reshape((CZ + 3) * 16, NY).T
            seen = product(split(part), plane_parts, NN)
            readings.append(jnp.sum(seen * weight_y, axis=0, keepdims=True))
        return readings

    lane = lax.broadcasted_iota(jnp.int32, (16, NY), 1)
    place = lax.broadcasted_iota(jnp.int32, (16, NY), 0)
    has_low_z, has_high_z = slab > 0, slab < slabs - 1
    own_x = (place >= 2) & (place < CX + 2)
    inside_x = own_x | ((place == CX + 2) & (tile < tiles - 1)) | ((place == 1) & (tile > 0))
    high_x = jnp.concatenate([(place < CX + 2) | (tile < tiles - 1)] * 3, axis=1)
    own_wide = jnp.concatenate([own_x] * 3, axis=1)

    def after_y(value):
        return jnp.where(lane == NY - 1, 0.0, pltpu.roll(value, NY - 1, 1))

    def before_y(value):
        return jnp.where(lane == 0, 0.0, pltpu.roll(value, 1, 1))

    def after_x(value):
        return pltpu.roll(value, 15, 0)

    def before_x(value):
        return pltpu.roll(value, 1, 0)

    def around(below, middle, above):
        total = (above + below) + (after_x(middle) + before_x(middle))
        return total + (after_y(middle) + before_y(middle)) - 6.0 * middle

    def cell(turn, c, z):
        return field[turn, z + 2, :, c * NY : (c + 1) * NY]

    def inside(value, z):
        keep = inside_x
        if z < 0:
            keep = keep & has_low_z
        if z >= CZ:
            keep = keep & has_high_z
        return jnp.where(keep, value, 0.0)

    def smooth(turn):
        for c in range(3):
            for z in range(-1, CZ + 1):
                value = around(cell(turn, c, z - 1), cell(turn, c, z), cell(turn, c, z + 1))
                bent[turn, c, z + 1] = inside(value, z)
        for z in range(-1, CZ):
            along_z = cell(turn, 0, z + 1) - cell(turn, 0, z)
            along_x = after_x(cell(turn, 1, z)) - cell(turn, 1, z)
            along_y = after_y(cell(turn, 2, z)) - cell(turn, 2, z)
            source[turn, z + 1] = inside(along_z + along_x + along_y, z)

    div_weight = div_ref[0]
    bend_weight = bend_ref[0]

    def penalties(turn, c, z):
        here = source[turn, z + 1]
        if c == 0:
            pushed = source[turn, z] - here
        elif c == 1:
            pushed = before_x(here) - here
        else:
            pushed = before_y(here) - here
        again = around(bent[turn, c, z], bent[turn, c, z + 1], bent[turn, c, z + 2])
        return jnp.where(own_x, div_weight * pushed + bend_weight * again, 0.0)

    def all_penalties(turn):
        return [
            jnp.concatenate([penalties(turn, c, z) for c in range(3)], axis=1) for z in range(CZ)
        ]

    def one(values, keep=None):
        value = functools.reduce(jnp.add, values)
        if keep is not None:
            value = jnp.where(keep, value, 0.0)
        return jnp.sum(jnp.sum(value, axis=0, keepdims=True), axis=1, keepdims=True)

    row_lane = lax.broadcasted_iota(jnp.int32, (1, LANES), 1)

    def sum_copy(turn, stage, step, incoming):
        buffer, size, mine, peer = (
            (sum_slab, slabs, slab, other_slab(step)) if stage == 0 else (sum_tile, tiles, tile, other_tile(step))
        )
        received = sum_slab_recv if stage == 0 else sum_tile_recv
        where = peer if incoming else mine
        return pltpu.make_async_remote_copy(
            src_ref=buffer.at[turn, pl.ds(mine, 1)], dst_ref=buffer.at[turn, pl.ds(where, 1)],
            send_sem=sum_send.at[turn, stage, step], recv_sem=received.at[turn, where],
            device_id=mesh_at(peer, tile) if stage == 0 else mesh_at(slab, peer),
        )

    def start_sum(turn, values):
        row = jnp.zeros((1, LANES), F32)
        for number, value in enumerate(values):
            row = jnp.where(row_lane == number, value, row)
        sum_slab[turn, pl.ds(slab, 1)] = row
        for step in range(1, slabs):
            copy = sum_copy(turn, 0, step, False)
            copy.start()
            drains.append(copy.wait_send)

    def turn_sum(turn):
        for step in range(1, slabs):
            sum_copy(turn, 0, step, True).wait_recv()
        sum_tile[turn, pl.ds(tile, 1)] = jnp.sum(sum_slab[turn], axis=0, keepdims=True)
        for step in range(1, tiles):
            copy = sum_copy(turn, 1, step, False)
            copy.start()
            drains.append(copy.wait_send)

    def end_sum(turn, number):
        for step in range(1, tiles):
            sum_copy(turn, 1, step, True).wait_recv()
        row = jnp.sum(sum_tile[turn], axis=0, keepdims=True)
        return [row[:, i : i + 1] for i in range(number)]

    partial[0] = spread([owned[12 + c : 13 + c] for c in range(3)])
    send_wide(0)
    wait_wide(0)
    for z in range(CZ + 5):
        field[0, z] = in_grid(added_up(0, z), z - 2)
    start = [field[0, z + 2] for z in range(CZ)]

    read_start = read_samples(0)
    smooth(0)

    def energy(readings, sources, bends):
        seen = one([v * v for v in readings])
        pushed = one([v * v for v in sources], own_x)
        again = one([v * v for v in bends], own_x)
        return seen + div_weight * pushed + bend_weight * again

    def own_source(turn):
        return [source[turn, z + 1] for z in range(CZ)]

    def own_bent(turn):
        return [bent[turn, c, z + 1] for c in range(3) for z in range(CZ)]

    square = one([v * v for v in start], own_wide)
    start_sum(0, [square, energy(read_start, own_source(0), own_bent(0))])
    held = all_penalties(0)
    fresh = spread(read_start)
    for z in range(CZ + 3):
        partial[1, z] = fresh[z] + held[z] if z < CZ else fresh[z]
    send_wide(1)
    turn_sum(0)
    wait_wide(1)
    for z in range(CZ + 5):
        field[1, z] = in_grid(added_up(1, z), z - 2)
    image = [field[1, z + 2] for z in range(CZ)]

    read_image = read_samples(1)
    smooth(1)
    norm, curvature = end_sum(0, 2)
    step_size = norm / curvature
    left = [b - step_size * y for b, y in zip(start, image)]
    left_square = one([v * v for v in left], own_wide)
    left_image = one([v * y for v, y in zip(left, image)], own_wide)
    left_energy = energy(
        [a - step_size * b for a, b in zip(read_start, read_image)],
        [a - step_size * b for a, b in zip(own_source(0), own_source(1))],
        [a - step_size * b for a, b in zip(own_bent(0), own_bent(1))],
    )
    start_sum(1, [left_square, left_image, left_energy])
    partial[2] = spread(read_image)
    send_wide(2)
    held = all_penalties(1)
    turn_sum(1)
    wait_wide(2)
    second = [added_up(2, z + 2) + held[z] for z in range(CZ)]
    left_square, left_image, left_energy = end_sum(1, 3)

    ratio = left_square / norm
    bowed = left_energy + 2.0 * ratio * left_image + ratio * ratio * curvature
    step_next = left_square / bowed
    for z in range(CZ):
        direction = left[z] + ratio * start[z]
        pushed = (image[z] - step_size * second[z]) + ratio * image[z]
        answer = step_size * start[z] + step_next * direction
        rest = left[z] - step_next * pushed
        for c in range(3):
            solution_ref[c, z] = answer[2 : CX + 2, c * NY : (c + 1) * NY]
            residual_ref[c, z] = rest[2 : CX + 2, c * NY : (c + 1) * NY]

    finish()


def local(slabs, tiles, owner, block_base, spline_weights, measured, div_weight, bend_weight):
    devices = slabs * tiles
    count = owner.shape[0]
    vmem = pl.BlockSpec(memory_space=pltpu.VMEM)
    dma = pltpu.SemaphoreType.DMA
    wide = 3 * NY
    out = pltpu.VMEM((3, CZ, CX, NY), F32)
    return pl.pallas_call(
        functools.partial(kernel, slabs, tiles),
        out_shape=(out, out),
        in_specs=[pl.BlockSpec(memory_space=pltpu.HBM)] * 6,
        out_specs=(vmem, vmem),
        scratch_shapes=[
            pltpu.VMEM((1, count), jnp.int32),
            pltpu.VMEM((3, count), jnp.int32),
            pltpu.VMEM((12, count), F32),
            pltpu.VMEM((3, count), F32),
            pltpu.SMEM((1,), F32),
            pltpu.SMEM((1,), F32),
            dma((6,)),
            pltpu.VMEM((32, count), F32),
            pltpu.VMEM((slabs, tiles, LANES), F32),
            pltpu.VMEM((slabs, tiles, LANES), F32),
            pltpu.VMEM((devices, LANES), F32),
            pltpu.VMEM((devices, LANES), F32),
            pltpu.VMEM((3, CZ + 3, 16, wide), F32),
            pltpu.VMEM((2, 9, 16, wide), F32),
            pltpu.VMEM((2, 3, CZ + 2, 16, NY), F32),
            pltpu.VMEM((2, CZ + 1, 16, NY), F32),
            pltpu.VMEM((2, slabs, LANES), F32),
            pltpu.VMEM((2, tiles, LANES), F32),
            dma((slabs + tiles,)),
            dma((slabs,)),
            dma((tiles,)),
            dma((3, len(WIDE))),
            dma((3, len(WIDE))),
            dma((2, 2, max(slabs, tiles))),
            dma((2, slabs)),
            dma((2, tiles)),
        ]
        + [pltpu.VMEM((entry[1][1], 8, wide), F32) for entries in ROUNDS for entry in entries],
        compiler_params=pltpu.CompilerParams(collective_id=0, has_side_effects=True),
    )(owner.reshape(1, count), block_base, spline_weights, measured, div_weight, bend_weight)


def solution(mesh):
    placed = (
        P(("slab", "tile"), None),
        P(None, ("slab", "tile")),
        P(None, ("slab", "tile")),
        P(None, ("slab", "tile")),
        P(),
        P(),
    )
    sizes = dict(zip(mesh.axis_names, mesh.devices.shape))
    return jax.shard_map(
        functools.partial(local, sizes["slab"], sizes["tile"]),
        mesh=mesh,
        in_specs=placed,
        out_specs=(P(None, "slab", "tile", None), P(None, "slab", "tile", None)),
        check_vma=False,
    )
```

time: 50.6 us -> 44.5 us (0.88)
  Pallas kernels: 46.2 us -> 41 us
  local copies, waits for them, and re-layouts: 2.06 us -> 1.24 us
    pallas_call x1, Pallas kernels: 46.2 us -> 41 us  [local(): pl.pallas_call(functools.partial(kernel, slabs, tiles), out_shape=(out, o...]
    unnamed x4 -> x2, local copies, waits for them, and re-layouts: 2.06 us -> 1.24 us
where the time goes in v2:
time: 44.5 us; the launch traced here: 44.2 us
  Pallas kernels  41 us (92%)
  between operations  1.93 us (4%)
  local copies, waits for them, and re-layouts  1.24 us (3%)
    pallas_call x1, Pallas kernels, local(): pl.pallas_call(functools.partial(kernel, slabs, tiles), out_shape=(out, o...  41 us
    unnamed x2, local copies, waits for them, and re-layouts  1.24 us

profile of v2, /device:TPU:1, one launch (start us, length us, event | category | flops | bytes accessed | tf_op | source)
XLA Modules:
  0.0 44.2 jit_solution(1686287769836303699)
XLA Ops:
  1.9 41.0 %shard_map.77 = (f32[3,4,8,128]{3,2,1,0:T(8,128)S(1)}, f32[3,4,8,128]{3,2,1,0:T(8,128)S(1)}) custom-call(s32[1,256]{1,0:T(1,128)} %bitcast.1, s32[3,256]{1,0:T(4,128)} %base_in.1, f32[12,256]{1,0:T(8,128)} %spline_in.1, f32[3,256]{1,0:T(4,128)} %measured_in.1, f32[1]{0:T(128)S(6)} %copy.12.div_in, f32[1]{0:T(128)S(6)} %copy.13.bend_in), custom_call_target="tpu_custom_call" | custom-call | tf_op jit(solution)/shard_map/pallas_call | solution.py:450
  42.9 0.6 %copy.10 = f32[3,4,8,128]{3,2,1,0:T(8,128)} copy(f32[3,4,8,128]{3,2,1,0:T(8,128)S(1)} %get-tuple-element.2) | data formatting | bytes 98304
  43.5 0.6 %copy.11 = f32[3,4,8,128]{3,2,1,0:T(8,128)} copy(f32[3,4,8,128]{3,2,1,0:T(8,128)S(1)} %get-tuple-element.3) | data formatting | bytes 98304

commit v3 on v2

--- a/solution.py
+++ b/solution.py
@@ -61,9 +61,9 @@
     solution_ref, residual_ref,
     owner_ref, base_ref, spline_ref, measured_ref, div_ref, bend_ref, load_sem,
     pay, out_rows, by_slab, turned, by_tile,
-    partial, field, bent, source, sum_slab, sum_tile,
+    partial, field, bent, source,
     pass_send, pass_slab_recv, pass_tile_recv, wide_send, wide_recv,
-    sum_send, sum_slab_recv, sum_tile_recv,
+    sums, sum_sem,
     *landed,
 ):
     landed = (landed[: len(WIDE)], landed[len(WIDE) : 2 * len(WIDE)], landed[2 * len(WIDE) :])
@@ -332,41 +332,38 @@
 
     row_lane = lax.broadcasted_iota(jnp.int32, (1, LANES), 1)
 
-    def sum_copy(turn, stage, step, incoming):
-        buffer, size, mine, peer = (
-            (sum_slab, slabs, slab, other_slab(step)) if stage == 0 else (sum_tile, tiles, tile, other_tile(step))
-        )
-        received = sum_slab_recv if stage == 0 else sum_tile_recv
-        where = peer if incoming else mine
-        return pltpu.make_async_remote_copy(
-            src_ref=buffer.at[turn, pl.ds(mine, 1)], dst_ref=buffer.at[turn, pl.ds(where, 1)],
-            send_sem=sum_send.at[turn, stage, step], recv_sem=received.at[turn, where],
-            device_id=mesh_at(peer, tile) if stage == 0 else mesh_at(slab, peer),
-        )
-
-    def start_sum(turn, values):
+    def far_first():
+        def hops(i, j):
+            z, y, x = (i // 2) % 4, j // 4, j % 4
+            return sum(min(k, 4 - k) for k in (z, y, x))
+
+        steps = [(i, j) for i in range(slabs) for j in range(tiles) if i or j]
+        return sorted(steps, key=lambda step: -hops(*step))
+
+    me = slab * tiles + tile
+
+    def start_sum(values):
         row = jnp.zeros((1, LANES), F32)
         for number, value in enumerate(values):
             row = jnp.where(row_lane == number, value, row)
-        sum_slab[turn, pl.ds(slab, 1)] = row
-        for step in range(1, slabs):
-            copy = sum_copy(turn, 0, step, False)
-            copy.start()
-            drains.append(copy.wait_send)
-
-    def turn_sum(turn):
-        for step in range(1, slabs):
-            sum_copy(turn, 0, step, True).wait_recv()
-        sum_tile[turn, pl.ds(tile, 1)] = jnp.sum(sum_slab[turn], axis=0, keepdims=True)
-        for step in range(1, tiles):
-            copy = sum_copy(turn, 1, step, False)
-            copy.start()
-            drains.append(copy.wait_send)
-
-    def end_sum(turn, number):
-        for step in range(1, tiles):
-            sum_copy(turn, 1, step, True).wait_recv()
-        row = jnp.sum(sum_tile[turn], axis=0, keepdims=True)
+        sums[pl.ds(me, 1)] = row
+        by_step_slab = [other_slab(step) if step else slab for step in range(slabs)]
+        by_step_tile = [other_tile(step) if step else tile for step in range(tiles)]
+        for i, j in far_first():
+            pltpu.make_async_remote_copy(
+                src_ref=sums.at[pl.ds(me, 1)], dst_ref=sums.at[pl.ds(me, 1)],
+                send_sem=sum_sem.at[0], recv_sem=sum_sem.at[1],
+                device_id=mesh_at(by_step_slab[i], by_step_tile[j]),
+            ).start()
+
+    def every_wait(number):
+        others = sums.at[pl.ds(0, devices - 1)]
+        pltpu.make_async_copy(others, others, sum_sem.at[number]).wait()
+
+    def end_sum(number):
+        every_wait(1)
+        drains.append(lambda: every_wait(0))
+        row = jnp.sum(sums[...], axis=0, keepdims=True)
         return [row[:, i : i + 1] for i in range(number)]
 
     partial[0] = spread([owned[12 + c : 13 + c] for c in range(3)])
@@ -391,14 +388,12 @@
     def own_bent(turn):
         return [bent[turn, c, z + 1] for c in range(3) for z in range(CZ)]
 
-    square = one([v * v for v in start], own_wide)
-    start_sum(0, [square, energy(read_start, own_source(0), own_bent(0))])
     held = all_penalties(0)
     fresh = spread(read_start)
     for z in range(CZ + 3):
         partial[1, z] = fresh[z] + held[z] if z < CZ else fresh[z]
     send_wide(1)
-    turn_sum(0)
+    square = one([v * v for v in start], own_wide)
     wait_wide(1)
     for z in range(CZ + 5):
         field[1, z] = in_grid(added_up(1, z), z - 2)
@@ -406,33 +401,32 @@
 
     read_image = read_samples(1)
     smooth(1)
-    norm, curvature = end_sum(0, 2)
-    step_size = norm / curvature
-    left = [b - step_size * y for b, y in zip(start, image)]
-    left_square = one([v * v for v in left], own_wide)
-    left_image = one([v * y for v, y in zip(left, image)], own_wide)
-    left_energy = energy(
-        [a - step_size * b for a, b in zip(read_start, read_image)],
-        [a - step_size * b for a, b in zip(own_source(0), own_source(1))],
-        [a - step_size * b for a, b in zip(own_bent(0), own_bent(1))],
-    )
-    start_sum(1, [left_square, left_image, left_energy])
+    start_sum([
+        square,
+        one([v * y for v, y in zip(start, image)], own_wide),
+        one([y * y for y in image], own_wide),
+        energy(read_image, own_source(1), own_bent(1)),
+    ])
     partial[2] = spread(read_image)
     send_wide(2)
     held = all_penalties(1)
-    turn_sum(1)
     wait_wide(2)
     second = [added_up(2, z + 2) + held[z] for z in range(CZ)]
-    left_square, left_image, left_energy = end_sum(1, 3)
-
+    norm, curvature, image_square, image_energy = end_sum(4)
+
+    step_size = norm / curvature
+    left_square = step_size * step_size * image_square - norm
     ratio = left_square / norm
+    left_image = curvature - step_size * image_square
+    left_energy = left_image - step_size * (image_square - step_size * image_energy)
     bowed = left_energy + 2.0 * ratio * left_image + ratio * ratio * curvature
     step_next = left_square / bowed
     for z in range(CZ):
-        direction = left[z] + ratio * start[z]
+        left = start[z] - step_size * image[z]
+        direction = left + ratio * start[z]
         pushed = (image[z] - step_size * second[z]) + ratio * image[z]
         answer = step_size * start[z] + step_next * direction
-        rest = left[z] - step_next * pushed
+        rest = left - step_next * pushed
         for c in range(3):
             solution_ref[c, z] = answer[2 : CX + 2, c * NY : (c + 1) * NY]
             residual_ref[c, z] = rest[2 : CX + 2, c * NY : (c + 1) * NY]
@@ -469,16 +463,13 @@
             pltpu.VMEM((2, 9, 16, wide), F32),
             pltpu.VMEM((2, 3, CZ + 2, 16, NY), F32),
             pltpu.VMEM((2, CZ + 1, 16, NY), F32),
-            pltpu.VMEM((2, slabs, LANES), F32),
-            pltpu.VMEM((2, tiles, LANES), F32),
             dma((slabs + tiles,)),
             dma((slabs,)),
             dma((tiles,)),
             dma((3, len(WIDE))),
             dma((3, len(WIDE))),
-            dma((2, 2, max(slabs, tiles))),
-            dma((2, slabs)),
-            dma((2, tiles)),
+            pltpu.VMEM((devices, LANES), F32),
+            dma((2,)),
         ]
         + [pltpu.VMEM((entry[1][1], 8, wide), F32) for entries in ROUNDS for entry in entries],
         compiler_params=pltpu.CompilerParams(collective_id=0, has_side_effects=True),

time: 44.5 us -> 39.3 us (0.88)
  Pallas kernels: 41 us -> 35.9 us
    pallas_call x1, Pallas kernels: 41 us -> 35.9 us  [local(): pl.pallas_call(functools.partial(kernel, slabs, tiles), out_shape=(out, o...]
where the time goes in v3:
time: 39.3 us; the launch traced here: 39.1 us
  Pallas kernels  35.9 us (91%)
  between operations  1.93 us (5%)
  local copies, waits for them, and re-layouts  1.24 us (3%)
    pallas_call x1, Pallas kernels, local(): pl.pallas_call(functools.partial(kernel, slabs, tiles), out_shape=(out, o...  35.9 us
    unnamed x2, local copies, waits for them, and re-layouts  1.24 us

profile of v3, /device:TPU:1, one launch (start us, length us, event | category | flops | bytes accessed | tf_op | source)
XLA Modules:
  0.0 39.1 jit_solution(9669720868725013222)
XLA Ops:
  1.9 35.9 %shard_map.77 = (f32[3,4,8,128]{3,2,1,0:T(8,128)S(1)}, f32[3,4,8,128]{3,2,1,0:T(8,128)S(1)}) custom-call(s32[1,256]{1,0:T(1,128)} %bitcast.1, s32[3,256]{1,0:T(4,128)} %base_in.1, f32[12,256]{1,0:T(8,128)} %spline_in.1, f32[3,256]{1,0:T(4,128)} %measured_in.1, f32[1]{0:T(128)S(6)} %copy.12.div_in, f32[1]{0:T(128)S(6)} %copy.13.bend_in), custom_call_target="tpu_custom_call" | custom-call | tf_op jit(solution)/shard_map/pallas_call | solution.py:444
  37.8 0.6 %copy.10 = f32[3,4,8,128]{3,2,1,0:T(8,128)} copy(f32[3,4,8,128]{3,2,1,0:T(8,128)S(1)} %get-tuple-element.2) | data formatting | bytes 98304
  38.5 0.6 %copy.11 = f32[3,4,8,128]{3,2,1,0:T(8,128)} copy(f32[3,4,8,128]{3,2,1,0:T(8,128)S(1)} %get-tuple-element.3) | data formatting | bytes 98304

commit v4 on v3

--- a/solution.py
+++ b/solution.py
@@ -51,19 +51,18 @@
     return high, (value - high.astype(F32)).astype(BF16)
 
 
-def product(left, right, dims):
-    dot = functools.partial(lax.dot_general, dimension_numbers=dims, preferred_element_type=F32)
-    return dot(left[0], right[0]) + (dot(left[0], right[1]) + dot(left[1], right[0]))
+def wrapped(value, size):
+    return jnp.where(value >= size, value - size, value)
 
 
 def kernel(
     slabs, tiles, owner_in, base_in, spline_in, measured_in, div_in, bend_in,
-    solution_ref, residual_ref,
+    both_ref,
     owner_ref, base_ref, spline_ref, measured_ref, div_ref, bend_ref, load_sem,
     pay, out_rows, by_slab, turned, by_tile,
     partial, field, bent, source,
     pass_send, pass_slab_recv, pass_tile_recv, wide_send, wide_recv,
-    sums, sum_sem,
+    sums, sum_sem, row_in,
     *landed,
 ):
     landed = (landed[: len(WIDE)], landed[len(WIDE) : 2 * len(WIDE)], landed[2 * len(WIDE) :])
@@ -82,10 +81,10 @@
         return {"slab": s, "tile": t}
 
     def other_slab(step):
-        return lax.rem(slab + step, slabs)
+        return wrapped(slab + step, slabs)
 
     def other_tile(step):
-        return lax.rem(tile + step, tiles)
+        return wrapped(tile + step, tiles)
 
     loads = [
         pltpu.make_async_copy(source, target, load_sem.at[number])
@@ -97,10 +96,19 @@
     for load in loads:
         load.start()
 
+    across = 4 if tiles > 4 else 2
+    column, line = lax.rem(tile, across), lax.div(tile, across)
+    lines = tiles // across
+    row_mates = [line * across + wrapped(column + step, across) for step in range(1, across)]
+    column_mates = [wrapped(tile + step * across, tiles) for step in range(1, lines)]
     for step in range(1, slabs):
         pl.semaphore_signal(barrier, inc=1, device_id=mesh_at(other_slab(step), tile))
-    for step in range(1, tiles):
-        pl.semaphore_signal(barrier, inc=1, device_id=mesh_at(slab, other_tile(step)))
+    for mate in row_mates + column_mates:
+        pl.semaphore_signal(barrier, inc=1, device_id=mesh_at(slab, mate))
+
+    def far(step):
+        x, y = step % 4, step // 4
+        return -(min(x, 4 - x) + min(y, tiles // 4 - y))
 
     for buffers in landed:
         for buffer in buffers:
@@ -129,9 +137,11 @@
     rows = [lax.dot_general(onehot_b, part, NT, preferred_element_type=F32) for part in (high, low, lowest)]
     out_rows[...] = ((rows[0] + rows[1]) + rows[2]).reshape(slabs, tiles, LANES)
 
-    pl.semaphore_wait(barrier, slabs - 1 + tiles - 1)
-
-    for step in range(1, slabs):
+    pl.semaphore_wait(barrier, slabs - 1 + across - 1 + lines - 1)
+    for mate in column_mates:
+        pl.semaphore_signal(row_in, inc=1, device_id=mesh_at(slab, mate))
+
+    for step in sorted(range(1, slabs), key=lambda step: -min(step, slabs - step)):
         to = other_slab(step)
         copy = pltpu.make_async_remote_copy(
             src_ref=out_rows.at[to], dst_ref=by_slab.at[slab],
@@ -150,7 +160,8 @@
         ).wait_recv()
     for s in range(slabs):
         turned[pl.ds(s, tiles, stride=slabs), :] = by_slab[s]
-    for step in range(1, tiles):
+    pl.semaphore_wait(row_in, lines - 1)
+    for step in sorted(range(1, tiles), key=far):
         to = other_tile(step)
         copy = pltpu.make_async_remote_copy(
             src_ref=turned.at[pl.ds(to * slabs, slabs)], dst_ref=by_tile.at[pl.ds(tile * slabs, slabs)],
@@ -183,11 +194,22 @@
     weight_x = spread_weights(16, 16, 4, 2)
     weight_y = spread_weights(NY, 17, 8)
     plane = jnp.concatenate([weight_z[z : z + 1] * weight_x for z in range(CZ + 3)], axis=0)
-    plane_parts = split(plane)
+    y_high, y_low = split(weight_y)
+    y_reading = jnp.concatenate([y_high, y_high, y_low], axis=0)
+    y_spreading = jnp.concatenate([y_high, y_high, y_low], axis=1)
+    rows = (CZ + 3) * 16
 
     def spread(values):
-        columns = split(jnp.concatenate([weight_y * values[c] for c in range(3)], axis=0))
-        return product(plane_parts, columns, NT).reshape(CZ + 3, 16, 3 * NY)
+        high, low = split(jnp.concatenate([plane * values[c] for c in range(3)], axis=0))
+        result = lax.dot_general(
+            jnp.concatenate([high, low, high], axis=1), y_spreading, NT, preferred_element_type=F32
+        )
+        return [
+            jnp.concatenate(
+                [result[c * rows + z * 16 : c * rows + z * 16 + 16] for c in range(3)], axis=1
+            )
+            for z in range(CZ + 3)
+        ]
 
     def exists(s, t):
         inside = None
@@ -206,7 +228,7 @@
             src_ref=partial.at[turn, pl.ds(z, zs), pl.ds(x + 2, xs)],
             dst_ref=landed[turn][number].at[pl.ds(0, zs), pl.ds(row, xs)],
             send_sem=wide_send.at[turn, number], recv_sem=wide_recv.at[turn, number],
-            device_id=mesh_at(lax.rem(slab + s + slabs, slabs), lax.rem(tile + t + tiles, tiles)),
+            device_id=mesh_at(wrapped(slab + s % slabs, slabs), wrapped(tile + t % tiles, tiles)),
         )
 
     def send_wide(turn):
@@ -252,12 +274,20 @@
         return jnp.where(keep, value, 0.0)
 
     def read_samples(turn):
-        readings = []
-        for c in range(3):
-            part = field[turn, 2 : CZ + 5, :, c * NY : (c + 1) * NY].reshape((CZ + 3) * 16, NY).T
-            seen = product(split(part), plane_parts, NN)
-            readings.append(jnp.sum(seen * weight_y, axis=0, keepdims=True))
-        return readings
+        values = jnp.concatenate(
+            [
+                field[turn, 2 : CZ + 5, :, c * NY : (c + 1) * NY].reshape(rows, NY)
+                for c in range(3)
+            ],
+            axis=0,
+        )
+        high, low = split(values)
+        seen = lax.dot_general(
+            jnp.concatenate([high, low, high], axis=1), y_reading, NN, preferred_element_type=F32
+        )
+        return [
+            jnp.sum(seen[c * rows : (c + 1) * rows] * plane, axis=0, keepdims=True) for c in range(3)
+        ]
 
     lane = lax.broadcasted_iota(jnp.int32, (16, NY), 1)
     place = lax.broadcasted_iota(jnp.int32, (16, NY), 0)
@@ -294,12 +324,14 @@
             keep = keep & has_high_z
         return jnp.where(keep, value, 0.0)
 
-    def smooth(turn):
+    def smooth(turn, layers):
         for c in range(3):
-            for z in range(-1, CZ + 1):
+            for z in layers:
                 value = around(cell(turn, c, z - 1), cell(turn, c, z), cell(turn, c, z + 1))
                 bent[turn, c, z + 1] = inside(value, z)
-        for z in range(-1, CZ):
+        for z in layers:
+            if z == CZ:
+                continue
             along_z = cell(turn, 0, z + 1) - cell(turn, 0, z)
             along_x = after_x(cell(turn, 1, z)) - cell(turn, 1, z)
             along_y = after_y(cell(turn, 2, z)) - cell(turn, 2, z)
@@ -332,41 +364,62 @@
 
     row_lane = lax.broadcasted_iota(jnp.int32, (1, LANES), 1)
 
-    def far_first():
-        def hops(i, j):
-            z, y, x = (i // 2) % 4, j // 4, j % 4
-            return sum(min(k, 4 - k) for k in (z, y, x))
-
-        steps = [(i, j) for i in range(slabs) for j in range(tiles) if i or j]
-        return sorted(steps, key=lambda step: -hops(*step))
-
     me = slab * tiles + tile
+
+    def distance(step):
+        i, j = step
+        return sum(
+            min(k, size - k)
+            for k, size in ((i // 2, slabs // 2), (j // 4, max(1, tiles // 4)), (j % 4, 4))
+        )
+
+    every = [(i, j) for i in range(slabs) for j in range(tiles) if i or j]
+    opposite = {(i, j): (-i % slabs, -j % tiles) for i, j in every}
+    paired = sorted([step for step in every if step < opposite[step]], key=lambda step: -distance(step))
+    alone = [step for step in every if step == opposite[step]]
+    middle = len(paired) // 2
+
+    def send_row(i, j):
+        pltpu.make_async_remote_copy(
+            src_ref=sums.at[pl.ds(me, 1)], dst_ref=sums.at[pl.ds(me, 1)],
+            send_sem=sum_sem.at[0], recv_sem=sum_sem.at[1],
+            device_id=mesh_at(wrapped(slab + i, slabs), wrapped(tile + j, tiles)),
+        ).start()
+
+    def send_rows(steps):
+        def body(turn, carry):
+            for i, j in steps:
+                send_row(
+                    jnp.where(turn == 0, i, -i % slabs), jnp.where(turn == 0, j, -j % tiles)
+                )
+            return carry
+
+        lax.fori_loop(0, 2, body, 0)
 
     def start_sum(values):
         row = jnp.zeros((1, LANES), F32)
         for number, value in enumerate(values):
             row = jnp.where(row_lane == number, value, row)
         sums[pl.ds(me, 1)] = row
-        by_step_slab = [other_slab(step) if step else slab for step in range(slabs)]
-        by_step_tile = [other_tile(step) if step else tile for step in range(tiles)]
-        for i, j in far_first():
-            pltpu.make_async_remote_copy(
-                src_ref=sums.at[pl.ds(me, 1)], dst_ref=sums.at[pl.ds(me, 1)],
-                send_sem=sum_sem.at[0], recv_sem=sum_sem.at[1],
-                device_id=mesh_at(by_step_slab[i], by_step_tile[j]),
-            ).start()
+        send_rows(paired[:middle])
+
+    def go_on_sum():
+        for step in alone:
+            send_row(*step)
+        send_rows(paired[middle:])
 
     def every_wait(number):
         others = sums.at[pl.ds(0, devices - 1)]
         pltpu.make_async_copy(others, others, sum_sem.at[number]).wait()
 
     def end_sum(number):
+        every_wait(0)
         every_wait(1)
-        drains.append(lambda: every_wait(0))
         row = jnp.sum(sums[...], axis=0, keepdims=True)
         return [row[:, i : i + 1] for i in range(number)]
 
-    partial[0] = spread([owned[12 + c : 13 + c] for c in range(3)])
+    for z, value in enumerate(spread([owned[12 + c : 13 + c] for c in range(3)])):
+        partial[0, z] = value
     send_wide(0)
     wait_wide(0)
     for z in range(CZ + 5):
@@ -374,7 +427,7 @@
     start = [field[0, z + 2] for z in range(CZ)]
 
     read_start = read_samples(0)
-    smooth(0)
+    smooth(0, range(-1, CZ + 1))
 
     def energy(readings, sources, bends):
         seen = one([v * v for v in readings])
@@ -400,18 +453,22 @@
     image = [field[1, z + 2] for z in range(CZ)]
 
     read_image = read_samples(1)
-    smooth(1)
+    smooth(1, range(CZ))
     start_sum([
         square,
         one([v * y for v, y in zip(start, image)], own_wide),
         one([y * y for y in image], own_wide),
         energy(read_image, own_source(1), own_bent(1)),
     ])
-    partial[2] = spread(read_image)
+    for z, value in enumerate(spread(read_image)):
+        partial[2, z] = value
     send_wide(2)
+    go_on_sum()
+    smooth(1, (-1, CZ))
     held = all_penalties(1)
     wait_wide(2)
     second = [added_up(2, z + 2) + held[z] for z in range(CZ)]
+    finish()
     norm, curvature, image_square, image_energy = end_sum(4)
 
     step_size = norm / curvature
@@ -428,10 +485,8 @@
         answer = step_size * start[z] + step_next * direction
         rest = left - step_next * pushed
         for c in range(3):
-            solution_ref[c, z] = answer[2 : CX + 2, c * NY : (c + 1) * NY]
-            residual_ref[c, z] = rest[2 : CX + 2, c * NY : (c + 1) * NY]
-
-    finish()
+            both_ref[0, c, z] = answer[2 : CX + 2, c * NY : (c + 1) * NY]
+            both_ref[1, c, z] = rest[2 : CX + 2, c * NY : (c + 1) * NY]
 
 
 def local(slabs, tiles, owner, block_base, spline_weights, measured, div_weight, bend_weight):
@@ -440,12 +495,12 @@
     vmem = pl.BlockSpec(memory_space=pltpu.VMEM)
     dma = pltpu.SemaphoreType.DMA
     wide = 3 * NY
-    out = pltpu.VMEM((3, CZ, CX, NY), F32)
-    return pl.pallas_call(
+    out = pltpu.VMEM((2, 3, CZ, CX, NY), F32)
+    both = pl.pallas_call(
         functools.partial(kernel, slabs, tiles),
-        out_shape=(out, out),
+        out_shape=out,
         in_specs=[pl.BlockSpec(memory_space=pltpu.HBM)] * 6,
-        out_specs=(vmem, vmem),
+        out_specs=vmem,
         scratch_shapes=[
             pltpu.VMEM((1, count), jnp.int32),
             pltpu.VMEM((3, count), jnp.int32),
@@ -470,10 +525,12 @@
             dma((3, len(WIDE))),
             pltpu.VMEM((devices, LANES), F32),
             dma((2,)),
+            pltpu.SemaphoreType.REGULAR,
         ]
         + [pltpu.VMEM((entry[1][1], 8, wide), F32) for entries in ROUNDS for entry in entries],
         compiler_params=pltpu.CompilerParams(collective_id=0, has_side_effects=True),
     )(owner.reshape(1, count), block_base, spline_weights, measured, div_weight, bend_weight)
+    return both[0], both[1]
 
 
 def solution(mesh):

time: 39.3 us -> 37.5 us (0.954)
  Pallas kernels: 35.9 us -> 34.7 us
  local copies, waits for them, and re-layouts: 1.24 us -> 0.64 us
    unnamed x2 -> x0, local copies, waits for them, and re-layouts: 1.24 us -> none
    pallas_call x1, Pallas kernels: 35.9 us -> 34.7 us  [local(): pl.pallas_call(functools.partial(kernel, slabs, tiles), out_shape=out, in...]
    squeeze x0 -> x1, local copies, waits for them, and re-layouts: none -> 0.64 us  [local(): return (both[0], both[1])]
where the time goes in v4:
time: 37.5 us; the launch traced here: 37.3 us
  Pallas kernels  34.7 us (93%)
  between operations  1.93 us (5%)
  local copies, waits for them, and re-layouts  0.64 us (2%)
    pallas_call x1, Pallas kernels, local(): pl.pallas_call(functools.partial(kernel, slabs, tiles), out_shape=out, in...  34.7 us

profile of v4, /device:TPU:1, one launch (start us, length us, event | category | flops | bytes accessed | tf_op | source)
XLA Modules:
  0.0 37.3 jit_solution(7805085330413274007)
XLA Ops:
  1.9 34.7 %shard_map.77 = f32[2,3,4,8,128]{4,3,2,1,0:T(8,128)S(1)} custom-call(s32[1,256]{1,0:T(1,128)} %bitcast.5, s32[3,256]{1,0:T(4,128)} %base_in.1, f32[12,256]{1,0:T(8,128)} %spline_in.1, f32[3,256]{1,0:T(4,128)} %measured_in.1, f32[1]{0:T(128)S(6)} %copy.8.div_in, f32[1]{0:T(128)S(6)} %copy.9.bend_in), custom_call_target="tpu_custom_call" | custom-call | tf_op jit(solution)/shard_map/pallas_call | solution.py:499
  36.6 0.6 %slice_bitcast_fusion = (f32[3,4,8,128]{3,2,1,0:T(8,128)}, f32[3,4,8,128]{3,2,1,0:T(8,128)}) fusion(f32[2,3,4,8,128]{4,3,2,1,0:T(8,128)S(1)} %shard_map.77), kind=kLoop, calls=%fused_computation | loop fusion | bytes 196608 | tf_op jit(solution)/shard_map/squeeze | solution.py:533

commit v5 on v4

--- a/solution.py
+++ b/solution.py
@@ -402,8 +402,6 @@
             row = jnp.where(row_lane == number, value, row)
         sums[pl.ds(me, 1)] = row
         send_rows(paired[:middle])
-
-    def go_on_sum():
         for step in alone:
             send_row(*step)
         send_rows(paired[middle:])
@@ -463,7 +461,6 @@
     for z, value in enumerate(spread(read_image)):
         partial[2, z] = value
     send_wide(2)
-    go_on_sum()
     smooth(1, (-1, CZ))
     held = all_penalties(1)
     wait_wide(2)
@@ -478,12 +475,11 @@
     left_energy = left_image - step_size * (image_square - step_size * image_energy)
     bowed = left_energy + 2.0 * ratio * left_image + ratio * ratio * curvature
     step_next = left_square / bowed
+    forward = step_size + step_next * (1.0 + ratio)
+    backward = step_size * step_next
     for z in range(CZ):
-        left = start[z] - step_size * image[z]
-        direction = left + ratio * start[z]
-        pushed = (image[z] - step_size * second[z]) + ratio * image[z]
-        answer = step_size * start[z] + step_next * direction
-        rest = left - step_next * pushed
+        answer = forward * start[z] - backward * image[z]
+        rest = (start[z] - forward * image[z]) + backward * second[z]
         for c in range(3):
             both_ref[0, c, z] = answer[2 : CX + 2, c * NY : (c + 1) * NY]
             both_ref[1, c, z] = rest[2 : CX + 2, c * NY : (c + 1) * NY]

time: 37.5 us -> 36.9 us (0.984)
  Pallas kernels: 34.7 us -> 34.2 us
    pallas_call x1, Pallas kernels: 34.7 us -> 34.2 us  [local(): pl.pallas_call(functools.partial(kernel, slabs, tiles), out_shape=out, in...]
where the time goes in v5:
time: 36.9 us; the launch traced here: 36.7 us
  Pallas kernels  34.2 us (93%)
  between operations  1.93 us (5%)
  local copies, waits for them, and re-layouts  0.64 us (2%)
    pallas_call x1, Pallas kernels, local(): pl.pallas_call(functools.partial(kernel, slabs, tiles), out_shape=out, in...  34.2 us

profile of v5, /device:TPU:1, one launch (start us, length us, event | category | flops | bytes accessed | tf_op | source)
XLA Modules:
  0.0 36.7 jit_solution(8219072875566226299)
XLA Ops:
  1.9 34.2 %shard_map.77 = f32[2,3,4,8,128]{4,3,2,1,0:T(8,128)S(1)} custom-call(s32[1,256]{1,0:T(1,128)} %bitcast.5, s32[3,256]{1,0:T(4,128)} %base_in.1, f32[12,256]{1,0:T(8,128)} %spline_in.1, f32[3,256]{1,0:T(4,128)} %measured_in.1, f32[1]{0:T(128)S(6)} %copy.8.div_in, f32[1]{0:T(128)S(6)} %copy.9.bend_in), custom_call_target="tpu_custom_call" | custom-call | tf_op jit(solution)/shard_map/pallas_call | solution.py:495
  36.1 0.6 %slice_bitcast_fusion = (f32[3,4,8,128]{3,2,1,0:T(8,128)}, f32[3,4,8,128]{3,2,1,0:T(8,128)}) fusion(f32[2,3,4,8,128]{4,3,2,1,0:T(8,128)S(1)} %shard_map.77), kind=kLoop, calls=%fused_computation | loop fusion | bytes 196608 | tf_op jit(solution)/shard_map/squeeze | solution.py:529

commit v6 on v5

--- a/solution.py
+++ b/solution.py
@@ -1,4 +1,5 @@
 import functools
+import itertools
 
 import jax
 import jax.numpy as jnp
@@ -86,6 +87,16 @@
     def other_tile(step):
         return wrapped(tile + step, tiles)
 
+    across = 4 if tiles > 4 else 2
+    column, line = lax.rem(tile, across), lax.div(tile, across)
+    lines = tiles // across
+    row_mates = [line * across + wrapped(column + step, across) for step in range(1, across)]
+    column_mates = [wrapped(tile + step * across, tiles) for step in range(1, lines)]
+    for step in sorted(range(1, slabs), key=lambda step: -min(step, slabs - step)):
+        pl.semaphore_signal(barrier, inc=1, device_id=mesh_at(other_slab(step), tile))
+    for mate in row_mates + column_mates:
+        pl.semaphore_signal(barrier, inc=1, device_id=mesh_at(slab, mate))
+
     loads = [
         pltpu.make_async_copy(source, target, load_sem.at[number])
         for number, (source, target) in enumerate((
@@ -95,16 +106,6 @@
     ]
     for load in loads:
         load.start()
-
-    across = 4 if tiles > 4 else 2
-    column, line = lax.rem(tile, across), lax.div(tile, across)
-    lines = tiles // across
-    row_mates = [line * across + wrapped(column + step, across) for step in range(1, across)]
-    column_mates = [wrapped(tile + step * across, tiles) for step in range(1, lines)]
-    for step in range(1, slabs):
-        pl.semaphore_signal(barrier, inc=1, device_id=mesh_at(other_slab(step), tile))
-    for mate in row_mates + column_mates:
-        pl.semaphore_signal(barrier, inc=1, device_id=mesh_at(slab, mate))
 
     def far(step):
         x, y = step % 4, step // 4
@@ -366,32 +367,39 @@
 
     me = slab * tiles + tile
 
+    sizes = (slabs // 2, 2, lines, across)
+    here = (lax.div(slab, 2), lax.rem(slab, 2), line, column)
+
+    def opposite(step):
+        return tuple(-k % size for k, size in zip(step, sizes))
+
     def distance(step):
-        i, j = step
-        return sum(
-            min(k, size - k)
-            for k, size in ((i // 2, slabs // 2), (j // 4, max(1, tiles // 4)), (j % 4, 4))
-        )
-
-    every = [(i, j) for i in range(slabs) for j in range(tiles) if i or j]
-    opposite = {(i, j): (-i % slabs, -j % tiles) for i, j in every}
-    paired = sorted([step for step in every if step < opposite[step]], key=lambda step: -distance(step))
-    alone = [step for step in every if step == opposite[step]]
-    middle = len(paired) // 2
-
-    def send_row(i, j):
-        pltpu.make_async_remote_copy(
-            src_ref=sums.at[pl.ds(me, 1)], dst_ref=sums.at[pl.ds(me, 1)],
-            send_sem=sum_sem.at[0], recv_sem=sum_sem.at[1],
-            device_id=mesh_at(wrapped(slab + i, slabs), wrapped(tile + j, tiles)),
-        ).start()
-
-    def send_rows(steps):
+        return sum(min(k, size - k) for k, size in zip(step[:1] + step[2:], sizes[:1] + sizes[2:])) + 0.1 * step[1]
+
+    every = list(itertools.product(*(range(size) for size in sizes)))[1:]
+    paired = sorted([step for step in every if step < opposite(step)], key=lambda step: -distance(step))
+    alone = [step for step in every if step == opposite(step)]
+
+    def send_rows(steps, turn):
+        def at(axis, k):
+            forward = wrapped(here[axis] + k, sizes[axis]) if k else here[axis]
+            k = -k % sizes[axis]
+            backward = wrapped(here[axis] + k, sizes[axis]) if k else here[axis]
+            return forward if turn is None else jnp.where(turn == 0, forward, backward)
+
+        z, core, y, x = ([at(axis, k) for k in range(sizes[axis])] for axis in range(4))
+        to_slab = {(i, j): z[i] * 2 + core[j] for i in range(sizes[0]) for j in range(2)}
+        to_tile = {(i, j): y[i] * across + x[j] for i in range(lines) for j in range(across)}
+        for step in steps:
+            pltpu.make_async_remote_copy(
+                src_ref=sums.at[pl.ds(me, 1)], dst_ref=sums.at[pl.ds(me, 1)],
+                send_sem=sum_sem.at[0], recv_sem=sum_sem.at[1],
+                device_id=mesh_at(to_slab[step[:2]], to_tile[step[2:]]),
+            ).start()
+
+    def send_pairs(steps):
         def body(turn, carry):
-            for i, j in steps:
-                send_row(
-                    jnp.where(turn == 0, i, -i % slabs), jnp.where(turn == 0, j, -j % tiles)
-                )
+            send_rows(steps, turn)
             return carry
 
         lax.fori_loop(0, 2, body, 0)
@@ -401,17 +409,18 @@
         for number, value in enumerate(values):
             row = jnp.where(row_lane == number, value, row)
         sums[pl.ds(me, 1)] = row
-        send_rows(paired[:middle])
-        for step in alone:
-            send_row(*step)
-        send_rows(paired[middle:])
+        far_alone = [step for step in alone if distance(step) > 3]
+        send_rows(far_alone, None)
+        middle = len(paired) // 2
+        send_pairs(paired[:middle])
+        send_pairs(paired[middle:])
+        send_rows([step for step in alone if step not in far_alone], None)
 
     def every_wait(number):
         others = sums.at[pl.ds(0, devices - 1)]
         pltpu.make_async_copy(others, others, sum_sem.at[number]).wait()
 
     def end_sum(number):
-        every_wait(0)
         every_wait(1)
         row = jnp.sum(sums[...], axis=0, keepdims=True)
         return [row[:, i : i + 1] for i in range(number)]
@@ -483,6 +492,8 @@
         for c in range(3):
             both_ref[0, c, z] = answer[2 : CX + 2, c * NY : (c + 1) * NY]
             both_ref[1, c, z] = rest[2 : CX + 2, c * NY : (c + 1) * NY]
+
+    every_wait(0)
 
 
 def local(slabs, tiles, owner, block_base, spline_weights, measured, div_weight, bend_weight):

time: 36.9 us -> 36.7 us (level)
  no operation moved by 1% of the time
where the time goes in v6:
time: 36.7 us; the launch traced here: 36.5 us
  Pallas kernels  33.9 us (92%)
  between operations  1.93 us (5%)
  local copies, waits for them, and re-layouts  0.64 us (2%)
    pallas_call x1, Pallas kernels, local(): pl.pallas_call(functools.partial(kernel, slabs, tiles), out_shape=out, in...  33.9 us

profile of v6, /device:TPU:1, one launch (start us, length us, event | category | flops | bytes accessed | tf_op | source)
XLA Modules:
  0.0 36.5 jit_solution(11394381307667618136)
XLA Ops:
  1.9 33.9 %shard_map.77 = f32[2,3,4,8,128]{4,3,2,1,0:T(8,128)S(1)} custom-call(s32[1,256]{1,0:T(1,128)} %bitcast.5, s32[3,256]{1,0:T(4,128)} %base_in.1, f32[12,256]{1,0:T(8,128)} %spline_in.1, f32[3,256]{1,0:T(4,128)} %measured_in.1, f32[1]{0:T(128)S(6)} %copy.8.div_in, f32[1]{0:T(128)S(6)} %copy.9.bend_in), custom_call_target="tpu_custom_call" | custom-call | tf_op jit(solution)/shard_map/pallas_call | solution.py:506
  35.9 0.6 %slice_bitcast_fusion = (f32[3,4,8,128]{3,2,1,0:T(8,128)}, f32[3,4,8,128]{3,2,1,0:T(8,128)}) fusion(f32[2,3,4,8,128]{4,3,2,1,0:T(8,128)S(1)} %shard_map.77), kind=kLoop, calls=%fused_computation | loop fusion | bytes 196608 | tf_op jit(solution)/shard_map/squeeze | solution.py:540

commit v7 on v6

--- a/solution.py
+++ b/solution.py
@@ -108,8 +108,8 @@
         load.start()
 
     def far(step):
-        x, y = step % 4, step // 4
-        return -(min(x, 4 - x) + min(y, tiles // 4 - y))
+        x, y = step % across, step // across
+        return -(min(x, across - x) + min(y, lines - y))
 
     for buffers in landed:
         for buffer in buffers:
@@ -163,7 +163,7 @@
         turned[pl.ds(s, tiles, stride=slabs), :] = by_slab[s]
     pl.semaphore_wait(row_in, lines - 1)
     for step in sorted(range(1, tiles), key=far):
-        to = other_tile(step)
+        to = wrapped(line + step // across, lines) * across + wrapped(column + step % across, across)
         copy = pltpu.make_async_remote_copy(
             src_ref=turned.at[pl.ds(to * slabs, slabs)], dst_ref=by_tile.at[pl.ds(tile * slabs, slabs)],
             send_sem=pass_send.at[slabs + step], recv_sem=pass_tile_recv.at[tile],

time: 36.7 us -> 36.7 us (level)
  no operation moved by 1% of the time
where the time goes in v7:
time: 36.7 us; the launch traced here: 36.5 us
  Pallas kernels  33.9 us (92%)
  between operations  1.93 us (5%)
  local copies, waits for them, and re-layouts  0.64 us (2%)
    pallas_call x1, Pallas kernels, local(): pl.pallas_call(functools.partial(kernel, slabs, tiles), out_shape=out, in...  33.9 us

profile of v7, /device:TPU:1, one launch (start us, length us, event | category | flops | bytes accessed | tf_op | source)
XLA Modules:
  0.0 36.5 jit_solution(7629606237331648783)
XLA Ops:
  1.9 33.9 %shard_map.77 = f32[2,3,4,8,128]{4,3,2,1,0:T(8,128)S(1)} custom-call(s32[1,256]{1,0:T(1,128)} %bitcast.5, s32[3,256]{1,0:T(4,128)} %base_in.1, f32[12,256]{1,0:T(8,128)} %spline_in.1, f32[3,256]{1,0:T(4,128)} %measured_in.1, f32[1]{0:T(128)S(6)} %copy.8.div_in, f32[1]{0:T(128)S(6)} %copy.9.bend_in), custom_call_target="tpu_custom_call" | custom-call | tf_op jit(solution)/shard_map/pallas_call | solution.py:506
  35.9 0.6 %slice_bitcast_fusion = (f32[3,4,8,128]{3,2,1,0:T(8,128)}, f32[3,4,8,128]{3,2,1,0:T(8,128)}) fusion(f32[2,3,4,8,128]{4,3,2,1,0:T(8,128)S(1)} %shard_map.77), kind=kLoop, calls=%fused_computation | loop fusion | bytes 196608 | tf_op jit(solution)/shard_map/squeeze | solution.py:540
